TPU v7x, 512 devices: a whole 4x4x16 slice. The times are simulated.
512 devices in a mesh: pairs: 64 (over x, z), grp: 8 (over y, core).
Axes of the slice: x: 4, y: 4, z: 16, core: 2. Of those that a mesh axis runs over, the one named last changes fastest.
Arguments:
- spectra: bfloat16 [8192, 1, 2048], P(('pairs', 'grp')), as said below
- row_station: int32 [8192], P(('pairs', 'grp')), may hold values from 0 to 4095, as said below
- row_window: int32 [8192], P(('pairs', 'grp')), may hold values from 0 to 1, as said below
- station_owner: int32 [4096], replicated, may hold values from 0 to 511, as said below
- tile_stations: int32 [64, 384], replicated, may hold values from 0 to 4095, as said below
- pair_index: int32 [64, 8, 2, 48], P('pairs', 'grp'), may hold values from 0 to 383
Outputs:
- correlation: float32 [64, 8, 48, 2001], P('pairs', 'grp')
Inputs may be any that keep to these rules, and one draw needn't show every extreme that they name: `row_station`: every station's 2 windows lie on the device that station_owner names, one row each; every device holds 8 stations. `row_window`: A device's rows of one station carry each window number once. `station_owner`: devices are numbered by pairs index times the size of grp plus grp index. `tile_stations`: A group's list holds distinct stations on distinct devices; exactly 48 of them lie on devices of each grp index. `spectra`: real parts of the 1024 bins, then their imaginary parts.
All inputs are finite; a program needn't handle non-finite values.
Results may differ from a plain program's by a relative error of at most 0.0056.
Values may be sent and summed in bfloat16 or wider, within the bound.
A program may use at most 64 MiB of HBM per device.

v0:
```python
import math

import jax
import jax.numpy as jnp
from jax import lax
from jax.sharding import PartitionSpec as P

W = 2
NSEG = 1
NFFT = 2048
BAND = 128
MAXLAG = 1000
LAGS = 2001


freq_block_max = 512
power_eps = 1e-06


def whiten_rows(spectra, band_width):
    half_bins = spectra.shape[-1] // 2
    leading = spectra.shape[:-1]
    values = spectra.astype(jnp.float32).reshape(leading + (2, half_bins // band_width, band_width))
    band_power = jnp.mean(jnp.sum(values * values, axis=-3), axis=-1)
    scaling = lax.rsqrt(band_power + power_eps)
    whitened = values * scaling[..., None, :, None]
    return whitened.reshape(spectra.shape).astype(jnp.bfloat16)


def lag_table(offset, bin_count):
    freq_index = (offset + jnp.arange(bin_count, dtype=jnp.int32))[:, None]
    lag_shift = (jnp.arange(LAGS, dtype=jnp.int32) + (NFFT - MAXLAG))[None, :]
    angles = (freq_index * lag_shift % NFFT).astype(jnp.float32) * (2.0 * math.pi / NFFT)
    return jnp.concatenate([jnp.cos(angles), -jnp.sin(angles)], axis=0).astype(jnp.bfloat16)


def cross_block(source_rows, first_rows, second_rows, offset, bin_count):
    half_bins = source_rows.shape[-1] // 2
    real_part = source_rows[:, :, offset : offset + bin_count]
    imag_part = source_rows[:, :, half_bins + offset : half_bins + offset + bin_count]
    real_a = real_part[first_rows].astype(jnp.float32)
    imag_a = imag_part[first_rows].astype(jnp.float32)
    real_b = real_part[second_rows].astype(jnp.float32)
    imag_b = imag_part[second_rows].astype(jnp.float32)
    cross_real = jnp.sum(real_a * real_b + imag_a * imag_b, axis=(1, 2))
    cross_imag = jnp.sum(imag_a * real_b - real_a * imag_b, axis=(1, 2))
    return jnp.concatenate([cross_real, cross_imag], axis=1).astype(jnp.bfloat16)


def correlate(source_rows, first_rows, second_rows):
    half_bins = NFFT // 2
    block_size = min(freq_block_max, half_bins)
    running = jnp.zeros((first_rows.shape[0], LAGS), jnp.float32)
    for offset in range(0, half_bins, block_size):
        cross_terms = cross_block(source_rows, first_rows, second_rows, offset, block_size)
        running = running + jnp.dot(
            cross_terms, lag_table(offset, block_size), preferred_element_type=jnp.float32
        )
    return running * (1.0 / math.sqrt(half_bins * W * NSEG))


def on_device(spectra, row_station, row_window, station_owner, tile_stations, pair_index):
    group_count = lax.axis_size("grp")
    pair_groups = lax.axis_size("pairs")
    my_pair = lax.axis_index("pairs")
    local_count = spectra.shape[0]
    row_tail = spectra.shape[1:]
    window_ids = jnp.arange(W, dtype=jnp.int32)
    local_ids = jnp.arange(local_count, dtype=jnp.int32)
    zero_value = jnp.zeros((), jnp.bfloat16)
    whitened = whiten_rows(spectra, BAND)
    my_tile = lax.dynamic_index_in_dim(tile_stations, my_pair, 0, keepdims=False)
    tile_owner = station_owner[my_tile]
    pooled, pooled_station, pooled_window = (
        lax.all_gather(whitened, "grp", axis=0, tiled=True),
        lax.all_gather(row_station, "grp", axis=0, tiled=True),
        lax.all_gather(row_window, "grp", axis=0, tiled=True),
    )
    wanted = jnp.any(pooled_station[None, :, None] == tile_stations[:, None, :], axis=2)
    wanted = wanted.reshape(pair_groups, group_count, 1, local_count)
    window_hit = (
        pooled_window.reshape(group_count, local_count)[:, None, :] == window_ids[None, :, None]
    )[None]
    selected = wanted & window_hit
    position = jnp.sum(jnp.where(selected, local_ids, 0), axis=3)
    position = position + (jnp.arange(group_count, dtype=jnp.int32) * local_count)[None, :, None]
    present = jnp.any(selected, axis=3)
    outgoing = jnp.where(present.reshape(-1, 1, 1), pooled[position.reshape(-1)], zero_value)
    outgoing = outgoing.reshape((pair_groups, group_count * W) + row_tail)
    arrived = lax.all_to_all(outgoing, "pairs", split_axis=0, concat_axis=0, tiled=True)
    source_rows = arrived.reshape((-1,) + row_tail)
    row_base = tile_owner * W
    pair_lists = pair_index.reshape(2, -1)
    first_rows = row_base[pair_lists[0]][:, None] + window_ids[None, :]
    second_rows = row_base[pair_lists[1]][:, None] + window_ids[None, :]
    running = correlate(source_rows, first_rows, second_rows)
    return running.reshape((pair_index.shape[0], pair_index.shape[1], pair_index.shape[3], LAGS))


def solution(mesh):
    placed = (
        P(("pairs", "grp"), None, None),
        P(("pairs", "grp")),
        P(("pairs", "grp")),
        P(),
        P(),
        P("pairs", "grp", None, None),
    )
    return jax.shard_map(
        on_device,
        mesh=mesh,
        in_specs=placed,
        out_specs=P("pairs", "grp", None, None),
        check_vma=False,
    )
```

profile of v0, /device:TPU:1, one launch (start us, length us, event | category | flops | bytes accessed | tf_op | source)
XLA Modules:
  0.0 266.3 jit_solution(16281639147075482824)
XLA Ops:
  0.0 1.3 dynamic-slice
  1.9 0.9 dynamic-update-slice.1
  2.8 0.8 dynamic-update-slice
  3.6 9.0 %all-reduce.2 = (s32[128]{0:T(128)S(1)}, s32[128]{0:T(128)S(1)}) all-reduce(s32[128]{0:T(128)S(1)} %dynamic-update-slice.1, s32[128]{0:T(128)S(1)} %dynamic-update-slice), channel_id=1, replica_groups=mesh['pairs'=64,'grp'=8] {'grp'}, use_global_device_ids=true, to_apply=%add.1 | all-reduce | flops 256 | bytes 2048
  12.7 2.1 compare_reduce_fusion
  15.3 0.9 fusion.30
  16.5 0.9 fusion.31
  17.8 17.5 %all_gather.11 = bf16[128,1,2048]{2,0,1:T(8,128)(2,1)S(1)} all-gather(bf16[16,1,2048]{2,0,1:T(8,128)(2,1)S(1)} %fusion.31), channel_id=1, replica_groups=mesh['pairs'=64,'grp'=8] {'grp'}, dimensions={0}, use_global_device_ids=true | all-gather | bytes 589824 | tf_op jit(solution)/shard_map/all_gather | solution.py:75
  35.3 6.0 %gather_fusion = bf16[1024,2048]{1,0:T(8,128)(2,1)} fusion(bf16[128,2048]{1,0:T(8,128)(2,1)S(1)} %bitcast.42, s32[1024]{0:T(1024)S(1)} %broadcast_clamp_fusion), kind=kCustom, calls=%fused_computation | custom fusion | bytes 8392704 | tf_op jit(solution)/shard_map/gather | solution.py:88
  41.3 4.5 %broadcast_select_fusion = bf16[64,16,1,2048]{3,1,2,0:T(8,128)(2,1)} fusion(bf16[64,16,1,2048]{3,1,2,0:T(8,128)(2,1)} %bitcast.43, pred[64,16]{1,0:T(8,128)(4,1)S(1)} %copy.17), kind=kLoop, calls=%fused_computation.42 | loop fusion | flops 2097152 | bytes 8389632 | tf_op jit(solution)/shard_map/jit(_where)/select_n | solution.py:88
  45.9 16.3 %all-to-all-start = ((bf16[64,16,1,2048]{3,1,2,0:T(8,128)(2,1)}), bf16[64,16,1,2048]{3,1,2,0:T(8,128)(2,1)}, u32[]{:S(2)}, u32[]{:S(2)}) async-start(bf16[64,16,1,2048]{3,1,2,0:T(8,128)(2,1)} %broadcast_select_fusion), calls=%async_computation | async-start | bytes 8388608 | tf_op jit(solution)/shard_map/all_to_all | solution.py:90
  62.9 2.5 gather_fusion.1
  65.5 0.8 gather_fusion.4
  66.3 0.8 gather_fusion.2
  67.5 36.1 %cosine_convert_fusion = (bf16[512,2001]{1,0:T(8,128)(2,1)}, bf16[512,2001]{1,0:T(8,128)(2,1)}, bf16[512,2001]{1,0:T(8,128)(2,1)}, bf16[512,2001]{1,0:T(8,128)(2,1)}) fusion(s32[2001]{0:T(1024)S(1)} %iota_add_fusion, s32[512]{0:T(512)S(1)} %iota_add_fusion.1), kind=kLoop, calls=%fused_computation.36 | loop fusion | flops 34833408 | bytes 8206148 | tf_op jit(solution)/shard_map/convert
  103.6 142.1 %all-to-all-done = bf16[64,16,1,2048]{3,1,2,0:T(8,128)(2,1)} async-done(((bf16[64,16,1,2048]{3,1,2,0:T(8,128)(2,1)}), bf16[64,16,1,2048]{3,1,2,0:T(8,128)(2,1)}, u32[]{:S(2)}, u32[]{:S(2)}) %all-to-all-start) | async-done | bytes 4194336 | tf_op jit(solution)/shard_map/all_to_all | solution.py:90
  245.8 3.6 %slice_bitcast_fusion = (bf16[1024,512]{1,0:T(8,128)(2,1)}, bf16[1024,512]{1,0:T(8,128)(2,1)S(1)}, bf16[1024,512]{1,0:T(8,128)(2,1)S(1)}, bf16[1024,512]{1,0:T(8,128)(2,1)S(1)}) fusion(bf16[1024,1,2048]{2,0,1:T(8,128)(2,1)} %bitcast.6), kind=kLoop, calls=%fused_computation.46 | loop fusion | bytes 8388608 | tf_op jit(solution)/shard_map/slice | solution.py:40
  249.4 2.2 gather_fusion.11
  251.5 2.2 gather_fusion.10
  254.5 1.4 gather_fusion.8
  256.7 0.8 gather_fusion.6
  259.0 1.0 fusion.28
  261.5 3.2 %fusion.6 = f32[48,2001]{1,0:T(8,128)S(1)} fusion(bf16[512,2001]{1,0:T(8,128)(2,1)} %get-tuple-element.17, bf16[512,2001]{1,0:T(8,128)(2,1)} %get-tuple-element.18, bf16[48,512]{1,0:T(8,128)(2,1)S(1)} %reduce_sum.61, bf16[48,512]{1,0:T(8,128)(2,1)S(1)} %reduce_sum.60), kind=kOutput, calls=%fused_computation.27 | convolution fusion | flops 205099008 | bytes 4580544 | tf_op jit(solution)/shard_map/dot_general | solution.py:56
  264.7 1.6 fusion.23
  (54 shorter events, 7.0 us)
Async XLA Ops:
  0.0 62.9 %copy-start = (s32[4096]{0:T(1024)S(1)}, s32[4096]{0:T(1024)}, u32[]{:S(2)}) copy-start(s32[4096]{0:T(1024)} %param.9) | copy-start | bytes 49156
  45.9 19.6 %copy-start.3 = (s32[1,1,2,48]{3,2,1,0:T(2,128)S(1)}, s32[1,1,2,48]{3,2,1,0:T(2,128)}, u32[]{:S(2)}) copy-start(s32[1,1,2,48]{3,2,1,0:T(2,128)} %param.11) | copy-start | bytes 1156
  45.9 199.9 %all-to-all-start = ((bf16[64,16,1,2048]{3,1,2,0:T(8,128)(2,1)}), bf16[64,16,1,2048]{3,1,2,0:T(8,128)(2,1)}, u32[]{:S(2)}, u32[]{:S(2)}) async-start(bf16[64,16,1,2048]{3,1,2,0:T(8,128)(2,1)} %broadcast_select_fusion), calls=%async_computation | async-start | bytes 8388608 | tf_op jit(solution)/shard_map/all_to_all | solution.py:90
  260.5 4.2 %copy-start.1 = (bf16[512,2001]{1,0:T(8,128)(2,1)S(1)}, bf16[512,2001]{1,0:T(8,128)(2,1)}, u32[]{:S(2)}) copy-start(bf16[512,2001]{1,0:T(8,128)(2,1)} %get-tuple-element.15) | copy-start | bytes 6147076
  261.5 3.2 %copy-start.2 = (bf16[512,2001]{1,0:T(8,128)(2,1)S(1)}, bf16[512,2001]{1,0:T(8,128)(2,1)}, u32[]{:S(2)}) copy-start(bf16[512,2001]{1,0:T(8,128)(2,1)} %get-tuple-element.16) | copy-start | bytes 6147076
where the time goes:
time: 269 us; the launch traced here: 266 us
  waiting for transfers between devices  142 us (53%)
  other arithmetic  47.8 us (18%)
  local copies, waits for them, and re-layouts  27.8 us (10%)
  blocking collectives  26.5 us (10%)
  starting transfers between devices  16.3 us (6%)
  matrix products  4.81 us (2%)
    all_to_all x1, waiting for transfers between devices, on_device(): lax.all_to_all(outgoing, 'pairs', split_axis=0, concat_axis=0, tiled=True)  142 us
    another operation x1, other arithmetic  36.1 us
    all_gather x1, blocking collectives, on_device(): lax.all_gather(whitened, 'grp', axis=0, tiled=True)  17.5 us
    all_to_all x1, starting transfers between devices, on_device(): lax.all_to_all(outgoing, 'pairs', split_axis=0, concat_axis=0, tiled=True)  16.3 us
    unnamed x1, blocking collectives  8.97 us
    gather x1, local copies, waits for them, and re-layouts, on_device(): pooled[position.reshape(-1)]  6.01 us
  transfers between devices with their start and end apart: 1, of which 1 were waited for; matrix products, arithmetic and copies ran while one was open for 16% of the time, Pallas kernels for 0%

commit v1 on v0

v1 whole, which is shorter than its diff:
```python
import math

import jax
import jax.numpy as jnp
from jax import lax
from jax.sharding import PartitionSpec as P

W = 2
NFFT = 2048
HALF = 1024
BAND = 128
BANDS = 8
MAXLAG = 1000
LAGS = 2001
power_eps = 1e-06


def whiten_rows(spectra):
    rows = spectra.shape[0]
    values = spectra.astype(jnp.float32).reshape(rows, 2, BANDS, BAND)
    band_power = jnp.mean(jnp.sum(values * values, axis=1), axis=-1)
    scaling = lax.rsqrt(band_power + power_eps)
    return (values * scaling[:, None, :, None]).astype(jnp.bfloat16)


def lag_table():
    freq = jnp.arange(HALF, dtype=jnp.int32)[:, None]
    step = 2.0 * math.pi / NFFT
    coarse = (jnp.arange(16, dtype=jnp.int32) * 128 + (NFFT - MAXLAG))[None, :]
    fine = jnp.arange(128, dtype=jnp.int32)[None, :]
    a = (freq * coarse % NFFT).astype(jnp.float32) * step
    b = (freq * fine % NFFT).astype(jnp.float32) * step
    ca, sa, cb, sb = lax.optimization_barrier((jnp.cos(a), jnp.sin(a), jnp.cos(b), jnp.sin(b)))
    ca, sa, cb, sb = ca[:, :, None], sa[:, :, None], cb[:, None, :], sb[:, None, :]
    real = (ca * cb - sa * sb).reshape(HALF, 2048)
    imag = -(sa * cb + ca * sb).reshape(HALF, 2048)
    table = jnp.stack([real.reshape(BANDS, BAND, 2048), imag.reshape(BANDS, BAND, 2048)], axis=1)
    return table.reshape(2 * HALF, 2048).astype(jnp.bfloat16)


def on_device(spectra, row_station, row_window, station_owner, tile_stations, pair_index):
    groups = lax.axis_size("pairs")
    members = lax.axis_size("grp")
    my_pair = lax.axis_index("pairs")
    local = spectra.shape[0]
    white = whiten_rows(spectra).reshape(local, 2 * HALF)
    wanted = jnp.any(row_station[None, :, None] == tile_stations[:, None, :], axis=2)
    window_hit = row_window[None, :] == jnp.arange(W, dtype=jnp.int32)[:, None]
    chosen = (wanted[:, None, :] & window_hit[None]).reshape(groups * W, local).astype(jnp.bfloat16)
    outgoing = jnp.dot(chosen, white, preferred_element_type=jnp.float32).astype(jnp.bfloat16)
    outgoing = outgoing.reshape(groups, W, 2, members, BAND).transpose(0, 3, 1, 2, 4)
    outgoing = outgoing.reshape(groups * members, W * 2 * BAND)
    arrived = lax.all_to_all(outgoing, ("pairs", "grp"), split_axis=0, concat_axis=0, tiled=True)
    pairs = pair_index.reshape(1, 2, -1)
    per_device = pairs.shape[2]
    pairs = lax.all_to_all(
        jnp.broadcast_to(pairs, (members,) + pairs.shape[1:]), "grp", split_axis=0, concat_axis=0, tiled=True
    )
    my_tile = lax.dynamic_index_in_dim(tile_stations, my_pair, 0, keepdims=False)
    owner = station_owner[my_tile]
    first = arrived[owner[pairs[:, 0].reshape(-1)]].astype(jnp.float32).reshape(-1, W, 2, BAND)
    second = arrived[owner[pairs[:, 1].reshape(-1)]].astype(jnp.float32).reshape(-1, W, 2, BAND)
    real = jnp.sum(first[:, :, 0] * second[:, :, 0] + first[:, :, 1] * second[:, :, 1], axis=1)
    imag = jnp.sum(first[:, :, 1] * second[:, :, 0] - first[:, :, 0] * second[:, :, 1], axis=1)
    cross = jnp.concatenate([real, imag], axis=1).astype(jnp.bfloat16)
    cross = cross.reshape(members, per_device, 2 * BAND)
    cross = lax.all_to_all(cross, "grp", split_axis=0, concat_axis=0, tiled=True)
    cross = cross.transpose(1, 0, 2).reshape(per_device, members * 2 * BAND)
    running = jnp.dot(cross, lag_table(), preferred_element_type=jnp.float32)[:, :LAGS]
    running = running * (1.0 / math.sqrt(HALF * W))
    return running.reshape(1, 1, per_device, LAGS)


def solution(mesh):
    placed = (
        P(("pairs", "grp"), None, None),
        P(("pairs", "grp")),
        P(("pairs", "grp")),
        P(),
        P(),
        P("pairs", "grp", None, None),
    )
    return jax.shard_map(
        on_device,
        mesh=mesh,
        in_specs=placed,
        out_specs=P("pairs", "grp", None, None),
        check_vma=False,
    )
```

time: 269 us -> 107 us (0.40)
  waiting for transfers between devices: 142 us -> 0.01 us
  blocking collectives: 26.5 us -> 0 us
  starting transfers between devices: 16.3 us -> 36.9 us
  other arithmetic: 47.8 us -> 30.2 us
  local copies, waits for them, and re-layouts: 27.8 us -> 31.9 us
    all_to_all x1 -> x3, waiting for transfers between devices: 142 us -> 0.01 us  [the longest x1 0.01 us: on_device(): lax.all_to_all(jnp.broadcast_to(pairs, (members,) + pairs.shape[1:]), 'gr...]
    all_to_all x1 -> x3, starting transfers between devices: 16.3 us -> 36.9 us  [the longest x1 19 us: on_device(): lax.all_to_all(outgoing, ('pairs', 'grp'), split_axis=0, concat_axis=0, t...]
    another operation x1 -> x2, other arithmetic: 36.1 us -> 17.5 us
    all_gather x1 -> x0, blocking collectives: 17.5 us -> none  [on_device(): lax.all_gather(whitened, 'grp', axis=0, tiled=True)]
    unnamed x1 -> x0, blocking collectives: 8.97 us -> none
    neg x0 -> x1, local copies, waits for them, and re-layouts: none -> 7.32 us  [lag_table(): imag = -(sa * cb + ca * sb).reshape(HALF, 2048)]
    gather x12 -> x5, local copies, waits for them, and re-layouts: 19.7 us -> 12.5 us  [the longest x1 2.8 us: on_device(): owner[pairs[:, 0].reshape(-1)]]
    sub x2 -> x1, local copies, waits for them, and re-layouts: 0.22 us -> 7.3 us  [lag_table(): real = (ca * cb - sa * sb).reshape(HALF, 2048)]
  transfers between devices with their start and end apart: 1 -> 3, of which waited for: 1 -> 0; matrix products, arithmetic and copies ran while one was open for 16% -> 50% of each run, Pallas kernels for 0% -> 0%
where the time goes in v1:
time: 107 us; the launch traced here: 106 us
  starting transfers between devices  36.9 us (34%)
  local copies, waits for them, and re-layouts  31.9 us (30%)
  other arithmetic  30.2 us (28%)
  matrix products  6.81 us (6%)
    all_to_all x1, starting transfers between devices, on_device(): lax.all_to_all(outgoing, ('pairs', 'grp'), split_axis=0, concat_axis=0, t...  19 us
    all_to_all x1, starting transfers between devices, on_device(): lax.all_to_all(jnp.broadcast_to(pairs, (members,) + pairs.shape[1:]), 'gr...  10.1 us
    another operation x1, other arithmetic  10.1 us
    all_to_all x1, starting transfers between devices, on_device(): lax.all_to_all(cross, 'grp', split_axis=0, concat_axis=0, tiled=True)  7.77 us
    another operation x1, other arithmetic, lag_table(): jnp.stack([real.reshape(BANDS, BAND, 2048), imag.reshape(BANDS, BAND, 204...  7.45 us
    neg x1, local copies, waits for them, and re-layouts, lag_table(): imag = -(sa * cb + ca * sb).reshape(HALF, 2048)  7.32 us
    sub x1, local copies, waits for them, and re-layouts, lag_table(): real = (ca * cb - sa * sb).reshape(HALF, 2048)  7.3 us
    dot_general x1, matrix products, on_device(): jnp.dot(cross, lag_table(), preferred_element_type=jnp.float32)[:, :LAGS]  5.7 us
  transfers between devices with their start and end apart: 3, of which 0 were waited for; matrix products, arithmetic and copies ran while one was open for 50% of the time, Pallas kernels for 0%

profile of v1, /device:TPU:1, one launch (start us, length us, event | category | flops | bytes accessed | tf_op | source)
XLA Modules:
  0.0 106.1 jit_solution(14028396341940244631)
XLA Ops:
  0.0 1.3 %broadcast_in_dim.5 = s32[8,2,48]{2,1,0:T(2,128)} broadcast(s32[2,48]{1,0:T(2,128)} %bitcast.44), dimensions={1,2} | broadcast | bytes 3456 | tf_op jit(solution)/shard_map/broadcast_in_dim | solution.py:57
  1.3 10.1 %all-to-all-start.1 = ((s32[8,2,48]{2,1,0:T(2,128)}), s32[8,2,48]{2,1,0:T(2,128)S(1)}, u32[]{:S(2)}, u32[]{:S(2)}) async-start(s32[8,2,48]{2,1,0:T(2,128)} %broadcast_in_dim.5), calls=%async_computation.1 | async-start | bytes 16384 | tf_op jit(solution)/shard_map/all_to_all | solution.py:56
  11.4 0.8 fusion.25
  13.2 2.1 %compare_reduce_fusion = pred[64,16]{1,0:T(8,128)(4,1)S(1)} fusion(s32[64,384]{1,0:T(8,128)} %param.10, s32[16]{0:T(128)} %param.7), kind=kLoop, calls=%fused_computation.13 | loop fusion | flops 785408 | bytes 99392 | tf_op jit(solution)/shard_map/reduce_or | solution.py:47
  15.4 1.1 %fusion.8 = bf16[16,8,16,128]{3,1,2,0:T(8,128)(2,1)S(1)} fusion(pred[128,16]{1,0:T(32,128)(4,1)S(1)} %and.41, f32[16,1,2048]{2,0,1:T(8,128)S(1)} %mul.188, bf16[16,1,2048]{2,0,1:T(8,128)(2,1)} %param.6), kind=kOutput, calls=%fused_computation.14 | convolution fusion | flops 8749056 | bytes 722944 | tf_op jit(solution)/shard_map/dot_general | solution.py:50
  17.2 1.1 %reduce.21 = bf16[512,512]{1,0:T(8,128)(2,1)S(1)} reduce(bf16[512,1,512]{2,0,1:T(8,128)(2,1)S(1)} %bitcast.38, bf16[]{:T(256)} %broadcast.211), dimensions={1}, to_apply=%copy.12.reduce_sub_computation | reduce | bytes 1048578 | tf_op jit(solution)/shard_map/all_to_all | solution.py:53
  18.3 0.9 reshape.363
  19.2 19.0 %all-to-all-start = ((bf16[512,2,256]{2,1,0:T(2,128)(2,1)}), bf16[512,2,256]{2,1,0:T(2,128)(2,1)S(1)}, u32[]{:S(2)}, u32[]{:S(2)}) async-start(bf16[512,2,256]{2,1,0:T(2,128)(2,1)} %reshape.363), calls=%async_computation | async-start | bytes 1048576 | tf_op jit(solution)/shard_map/all_to_all | solution.py:53
  38.3 2.1 %fusion.21 = (f32[1024,128]{1,0:T(8,128)S(1)}, f32[1024,128]{1,0:T(8,128)S(1)}) fusion(), kind=kLoop, calls=%fused_computation.36 | loop fusion | flops 1835008 | bytes 1048576 | tf_op jit(solution)/shard_map/sin | solution.py:33
  40.3 2.1 %fusion.23 = (f32[1024,16]{1,0:T(8,128)S(1)}, f32[1024,16]{1,0:T(8,128)S(1)}) fusion(s32[16]{0:T(128)S(1)} %multiply_add_fusion), kind=kLoop, calls=%fused_computation.38 | loop fusion | flops 229376 | bytes 131136 | tf_op jit(solution)/shard_map/sin | solution.py:33
  42.4 10.1 %subtract_convert_fusion = (bf16[1024,16,128]{2,1,0:T(8,128)(2,1)}, bf16[1024,16,128]{2,1,0:T(8,128)(2,1)}) fusion(f32[1024,128]{1,0:T(8,128)S(1)} %get-tuple-element.12, f32[1024,16]{1,0:T(8,128)S(1)} %get-tuple-element.11, f32[1024,128]{1,0:T(8,128)S(1)} %get-tuple-element.10, f32[1024,16]{1,0:T(8,128)S(1)} %get-tuple-element.9), kind=kLoop, calls=%fused_computation.9 | loop fusion | flops 18874368 | bytes 9568256 | tf_op jit(solution)/shard_map/convert.5
  52.4 7.3 %neg.14 = bf16[8,1,128,2048]{3,2,1,0:T(8,128)(2,1)} reshape(bf16[1024,16,128]{2,1,0:T(8,128)(2,1)} %get-tuple-element.18) | data formatting | bytes 8388608 | tf_op jit(solution)/shard_map/neg | solution.py:36
  59.8 7.3 %sub.19 = bf16[8,1,128,2048]{3,2,1,0:T(8,128)(2,1)} reshape(bf16[1024,16,128]{2,1,0:T(8,128)(2,1)} %get-tuple-element.17) | data formatting | bytes 8388608 | tf_op jit(solution)/shard_map/sub | solution.py:35
  67.1 0.7 fusion.29
  67.8 2.5 %gather_fusion = s32[384]{0:T(512)S(1)} fusion(s32[4096]{0:T(1024)S(1)} %copy-done, s32[1024]{0:T(1024)S(1)} %pad_clamp_fusion.4), kind=kCustom, calls=%fused_computation | custom fusion | bytes 4608 | tf_op jit(solution)/shard_map/gather | solution.py:60
  70.6 2.8 %gather_fusion.1 = s32[384]{0:T(512)S(1)} fusion(s32[384]{0:T(512)S(1)} %gather_fusion, s32[1024]{0:T(1024)S(1)} %pad_clamp_fusion.3), kind=kCustom, calls=%fused_computation.1 | custom fusion | bytes 4608 | tf_op jit(solution)/shard_map/gather | solution.py:61
  73.4 2.8 %gather_fusion.3 = s32[384]{0:T(512)S(1)} fusion(s32[384]{0:T(512)S(1)} %gather_fusion, s32[1024]{0:T(1024)S(1)} %pad_clamp_fusion.1), kind=kCustom, calls=%fused_computation.3 | custom fusion | bytes 4608 | tf_op jit(solution)/shard_map/gather | solution.py:62
  76.9 2.1 %gather_fusion.2 = bf16[384,512]{1,0:T(8,128)(2,1)S(1)} fusion(bf16[512,512]{1,0:T(8,128)(2,1)S(1)} %bitcast.35, s32[1024]{0:T(1024)S(1)} %pad_clamp_fusion.2), kind=kCustom, calls=%fused_computation.2 | custom fusion | bytes 787968 | tf_op jit(solution)/shard_map/gather | solution.py:61
  79.5 2.3 %gather_fusion.4 = bf16[384,512]{1,0:T(8,128)(2,1)S(1)} fusion(bf16[512,512]{1,0:T(8,128)(2,1)S(1)} %bitcast.36, s32[1024]{0:T(1024)S(1)} %pad_clamp_fusion), kind=kCustom, calls=%fused_computation.4 | custom fusion | bytes 787968 | tf_op jit(solution)/shard_map/gather | solution.py:62
  82.3 2.2 %add_reduce_fusion = (bf16[384,128]{1,0:T(8,128)(2,1)S(1)}, bf16[384,128]{1,0:T(8,128)(2,1)S(1)}) fusion(f32[384,2,2,128]{3,2,1,0:T(2,128)S(1)} %reshape.305, f32[384,2,2,128]{3,2,1,0:T(2,128)S(1)} %reshape.304), kind=kLoop, calls=%fused_computation.35 | loop fusion | flops 688128 | bytes 1769472 | tf_op jit(solution)/shard_map/reduce_sum | solution.py:63
  84.5 0.7 pad_maximum_fusion.1
  85.2 7.8 %all-to-all-start.2 = ((bf16[8,48,256]{2,1,0:T(8,128)(2,1)}), bf16[8,48,256]{2,1,0:T(8,128)(2,1)S(1)}, u32[]{:S(2)}, u32[]{:S(2)}) async-start(bf16[8,48,256]{2,1,0:T(8,128)(2,1)} %pad_maximum_fusion.1), calls=%async_computation.2 | async-start | bytes 393216 | tf_op jit(solution)/shard_map/all_to_all | solution.py:67
  92.9 7.5 %pad_maximum_fusion = bf16[8,2,128,2048]{3,2,1,0:T(8,128)(2,1)} fusion(bf16[8,1,128,2048]{3,2,1,0:T(8,128)(2,1)} %neg.14, bf16[8,1,128,2048]{3,2,1,0:T(8,128)(2,1)} %sub.19), kind=kLoop, calls=%fused_computation.7 | loop fusion | flops 4194304 | bytes 16777216 | tf_op jit(solution)/shard_map/stack | solution.py:37
  100.4 5.7 %fusion.5 = f32[1,1,48,2001]{3,2,1,0:T(8,128)} fusion(bf16[48,2048]{1,0:T(8,128)(2,1)S(1)} %bitcast.43, bf16[2048,2048]{1,0:T(8,128)(2,1)} %bitcast.37), kind=kOutput, calls=%fused_computation.12 | convolution fusion | flops 393508672 | bytes 8969408 | tf_op jit(solution)/shard_map/dot_general | solution.py:69
  (33 shorter events, 3.6 us)
Async XLA Ops:
  0.0 67.8 %copy-start = (s32[4096]{0:T(1024)S(1)}, s32[4096]{0:T(1024)}, u32[]{:S(2)}) copy-start(s32[4096]{0:T(1024)} %param.9) | copy-start | bytes 49156
  1.3 17.9 %all-to-all-start.1 = ((s32[8,2,48]{2,1,0:T(2,128)}), s32[8,2,48]{2,1,0:T(2,128)S(1)}, u32[]{:S(2)}, u32[]{:S(2)}) async-start(s32[8,2,48]{2,1,0:T(2,128)} %broadcast_in_dim.5), calls=%async_computation.1 | async-start | bytes 16384 | tf_op jit(solution)/shard_map/all_to_all | solution.py:56
  19.2 57.1 %all-to-all-start = ((bf16[512,2,256]{2,1,0:T(2,128)(2,1)}), bf16[512,2,256]{2,1,0:T(2,128)(2,1)S(1)}, u32[]{:S(2)}, u32[]{:S(2)}) async-start(bf16[512,2,256]{2,1,0:T(2,128)(2,1)} %reshape.363), calls=%async_computation | async-start | bytes 1048576 | tf_op jit(solution)/shard_map/all_to_all | solution.py:53
  85.2 15.2 %all-to-all-start.2 = ((bf16[8,48,256]{2,1,0:T(8,128)(2,1)}), bf16[8,48,256]{2,1,0:T(8,128)(2,1)S(1)}, u32[]{:S(2)}, u32[]{:S(2)}) async-start(bf16[8,48,256]{2,1,0:T(8,128)(2,1)} %pad_maximum_fusion.1), calls=%async_computation.2 | async-start | bytes 393216 | tf_op jit(solution)/shard_map/all_to_all | solution.py:67

commit v2 on v1

v2 whole, which is shorter than its diff:
```python
import math

import jax
import jax.numpy as jnp
from jax import lax
from jax.experimental import pallas as pl
from jax.experimental.pallas import tpu as pltpu
from jax.sharding import PartitionSpec as P

MESH = pl.DeviceIdType.MESH
W = 2
NFFT = 2048
HALF = 1024
MAXLAG = 1000
LAGS = 2001
EPS = 1e-06
NX = 4
NZ = 16
NG = 8
LAYER = NX * NG
STA = 8
PPD = 48
TOTAL = NZ * LAYER * STA
STEP = 2.0 * math.pi / NFFT
F32 = jnp.float32
I32 = jnp.int32
BF16 = jnp.bfloat16


def iota(shape, axis):
    return lax.broadcasted_iota(I32, shape, axis)


def angle(steps):
    return lax.rem(steps, NFFT).astype(F32) * STEP


def diagonal_column(row, size):
    same = iota((size, size), 0) == iota((size, size), 1)
    return jnp.sum(jnp.where(same, jnp.broadcast_to(row, (size, size)), 0), axis=1, keepdims=True)


def pack_rows(spec_ref, station_ref, window_ref, send_ref):
    station = station_ref[...]
    column = diagonal_column(station, 2 * STA)
    ahead = jnp.sum(jnp.where(column < station, 1, 0), axis=0, keepdims=True)
    place = window_ref[...] * STA + lax.div(ahead, W)
    order = jnp.where(iota((2 * STA, 2 * STA), 0) == place, 1.0, 0.0).astype(BF16)
    group = lax.div(iota((STA, 128), 1), 32)
    for tile in range(8):
        real = spec_ref[:, 128 * tile : 128 * tile + 128].astype(F32)
        imag = spec_ref[:, HALF + 128 * tile : HALF + 128 * tile + 128].astype(F32)
        power = jnp.sum(real * real + imag * imag, axis=1, keepdims=True) * (1.0 / 128)
        scale = lax.rsqrt(power + EPS)
        real = jnp.dot(order, (real * scale).astype(BF16), preferred_element_type=F32)
        imag = jnp.dot(order, (imag * scale).astype(BF16), preferred_element_type=F32)
        parts = (real[:STA], imag[:STA], real[STA:], imag[STA:])
        for quarter in range(4):
            piece = None
            for k in range(4):
                shift = (32 * (k - quarter)) % 128
                moved = pltpu.roll(parts[k], shift, 1) if shift else parts[k]
                piece = moved if piece is None else jnp.where(group == k, moved, piece)
            send_ref[4 * tile + quarter] = piece.astype(BF16)


def locate(pair_ref, tiles_ref, owner_ref, group):
    ends = 2 * PPD
    pairs = pair_ref[...]
    place = jnp.concatenate([diagonal_column(pairs[h : h + 1], PPD) for h in range(2)], axis=0)
    lanes = iota((ends, 128), 1)
    stations = tiles_ref[pl.ds(group, 1), :]
    found = jnp.zeros((ends, 128), I32)
    for c in range(3):
        found += jnp.where(place == lanes + 128 * c, stations[:, 128 * c : 128 * c + 128], 0)
    station = jnp.sum(found, axis=1, keepdims=True)
    found = jnp.zeros((ends, 128), I32)
    for c in range(32):
        found += jnp.where(station == lanes + 128 * c, owner_ref[c : c + 1, :], 0)
    owner = jnp.sum(found, axis=1, keepdims=True)
    found = jnp.zeros((ends, 128), I32)
    for c in range(32):
        ahead = (owner_ref[c : c + 1, :] == owner) & (lanes + 128 * c < station)
        found += jnp.where(ahead, 1, 0)
    rank = jnp.sum(found, axis=1, keepdims=True)
    part, member = lax.div(owner, NG), lax.rem(owner, NG)
    row = (lax.rem(part, NZ) * LAYER + lax.div(part, NZ) * NG + member) * STA + rank
    spread = jnp.where(iota((ends, 128), 0) == lanes, jnp.broadcast_to(row, (ends, 128)), 0)
    return jnp.sum(spread, axis=0, keepdims=True)


def build_table(table_ref, c8_ref, s8_ref, dc_ref, ds_ref):
    shift = NFFT - MAXLAG
    sub, lane = iota((8, 128), 0), iota((8, 128), 1)
    fine = angle(sub * (lane + shift))
    c0, s0 = jnp.cos(fine), jnp.sin(fine)
    coarse = angle(8 * iota((128, 128), 0) * (iota((128, 128), 1) + shift))
    c8_ref[...] = jnp.cos(coarse)
    s8_ref[...] = jnp.sin(coarse)
    for j in range(16):
        turn = angle(128 * j * sub)
        dc_ref[j] = jnp.cos(turn)
        ds_ref[j] = jnp.sin(turn)

    def block(u, carry):
        for h in range(2):
            base = []
            for q in range(2):
                v = 4 * u + 2 * h + q
                cv, sv = c8_ref[pl.ds(v, 1), :], s8_ref[pl.ds(v, 1), :]
                c, s = cv * c0 - sv * s0, sv * c0 + cv * s0
                base.append((c, s, -c, -s))
            for j in range(16):
                dc, ds = dc_ref[j], ds_ref[j]
                reals, imags = [], []
                for q in range(2):
                    c, s, nc, ns = base[q]
                    if q == 1 and j % 2 == 1:
                        c, s, nc, ns = nc, ns, c, s
                    reals.append(c * dc - s * ds)
                    imags.append(ns * dc + nc * ds)
                top = pl.multiple_of(64 * u + 16 * h, 16)
                low = pl.multiple_of(64 * u + 32 + 16 * h, 16)
                cols = slice(128 * j, 128 * j + 128)
                table_ref[pl.ds(top, 16), cols] = jnp.concatenate(reals, axis=0).astype(BF16)
                table_ref[pl.ds(low, 16), cols] = jnp.concatenate(imags, axis=0).astype(BF16)
        return carry

    lax.fori_loop(0, LAYER, block, 0)


def kernel(
    spec_ref, station_ref, window_ref, owner_ref, tiles_ref, pair_ref, out_ref,
    send_ref, rows_ref, wide_ref, index_ref, place_ref, first_ref, second_ref, cross_ref, got_ref, left_ref,
    table_ref, c8_ref, s8_ref, dc_ref, ds_ref,
    piece_send, piece_recv, index_send, index_recv, cross_send, cross_recv, ring_send, ring_recv, local_sem,
):
    group, member = lax.axis_index("pairs"), lax.axis_index("grp")
    x, z = lax.div(group, NZ), lax.rem(group, NZ)
    me = x * NG + member

    def device(number, layer):
        return (lax.div(number, NG) * NZ + layer, lax.rem(number, NG))

    def peer(j):
        return lax.rem(me + j, LAYER)

    ahead, behind = lax.rem(z + 1, NZ), lax.rem(z + NZ - 1, NZ)
    barrier = pltpu.get_barrier_semaphore()

    def greet(j, carry):
        pl.semaphore_signal(barrier, inc=1, device_id=device(peer(j), z), device_id_type=MESH)
        return carry

    lax.fori_loop(1, LAYER, greet, 0)
    pl.semaphore_signal(barrier, inc=1, device_id=device(me, ahead), device_id_type=MESH)
    pl.semaphore_signal(barrier, inc=1, device_id=device(me, behind), device_id_type=MESH)

    pack_rows(spec_ref, station_ref, window_ref, send_ref)
    index_ref[me] = locate(pair_ref, tiles_ref, owner_ref, group)
    rows_ref[z, me] = send_ref[me]
    pl.semaphore_wait(barrier, LAYER + 1)

    def piece_copy(number):
        return pltpu.make_async_remote_copy(
            src_ref=send_ref.at[number], dst_ref=rows_ref.at[z, me],
            send_sem=piece_send.at[number], recv_sem=piece_recv.at[me],
            device_id=device(number, z), device_id_type=MESH,
        )

    def piece_arrival(number):
        return pltpu.make_async_remote_copy(
            src_ref=send_ref.at[number], dst_ref=rows_ref.at[z, number],
            send_sem=piece_send.at[number], recv_sem=piece_recv.at[number],
            device_id=device(number, z), device_id_type=MESH,
        )

    def index_copy(number, source):
        return pltpu.make_async_remote_copy(
            src_ref=index_ref.at[me], dst_ref=index_ref.at[source],
            send_sem=index_send.at[number], recv_sem=index_recv.at[source],
            device_id=device(number, z), device_id_type=MESH,
        )

    def cross_copy(number, source):
        return pltpu.make_async_remote_copy(
            src_ref=cross_ref.at[number], dst_ref=got_ref.at[source],
            send_sem=cross_send.at[number], recv_sem=cross_recv.at[source],
            device_id=device(number, z), device_id_type=MESH,
        )

    def send_pieces(j, carry):
        piece_copy(peer(j)).start()
        return carry

    lax.fori_loop(1, LAYER, send_pieces, 0)

    def send_index(j, carry):
        index_copy(peer(j), me).start()
        return carry

    lax.fori_loop(1, LAYER, send_index, 0)

    build_table(table_ref, c8_ref, s8_ref, dc_ref, ds_ref)

    def ring_copy(way, d, s, chunk):
        part = pl.ds(NG * s, NG)
        return pltpu.make_async_remote_copy(
            src_ref=rows_ref.at[chunk, part], dst_ref=rows_ref.at[chunk, part],
            send_sem=ring_send.at[way, d, s], recv_sem=ring_recv.at[way, d, s],
            device_id=device(me, ahead if way == 0 else behind), device_id_type=MESH,
        )

    def widen(chunk, s):
        start = pl.multiple_of((chunk * LAYER + s * NG) * STA, 64)
        wide_ref[pl.ds(start, NG * STA), :] = rows_ref[chunk, pl.ds(NG * s, NG)].astype(F32).reshape(NG * STA, 128)

    def chunk_of(way, d):
        return lax.rem(z + NZ - d, NZ) if way == 0 else lax.rem(z + d, NZ)

    for k in range(NX):
        s = lax.rem(x + k, NX)

        def arrival(m, carry):
            number = s * NG + m

            @pl.when(number != me)
            def _():
                piece_arrival(number).wait_recv()

            return carry

        lax.fori_loop(0, NG, arrival, 0)
        ring_copy(0, 0, s, z).start()
        ring_copy(1, 0, s, z).start()
        widen(z, s)

    def index_arrival(j, carry):
        number = peer(j)
        index_copy(number, number).wait_recv()
        return carry

    lax.fori_loop(1, LAYER, index_arrival, 0)
    to_scalar = pltpu.make_async_copy(index_ref, place_ref, local_sem)
    to_scalar.start()

    def hop(d, carry):
        for k in range(NX):
            s = lax.rem(x + k, NX)
            for way in range(2):
                chunk = chunk_of(way, d + 1)
                ring_copy(way, d, s, chunk).wait_recv()
                ring_copy(way, d + 1, s, chunk).start()
                widen(chunk, s)
        return carry

    lax.fori_loop(0, 6, hop, 0)
    for k in range(NX):
        s = lax.rem(x + k, NX)
        for way in range(2):
            chunk = chunk_of(way, 7)
            ring_copy(way, 6, s, chunk).wait_recv()
            if (k < 2) == (way == 0):
                ring_copy(way, 7, s, chunk).start()
            widen(chunk, s)
    for k in range(NX):
        s = lax.rem(x + k, NX)
        way = 0 if k < 2 else 1
        chunk = chunk_of(way, 8)
        ring_copy(way, 7, s, chunk).wait_recv()
        widen(chunk, s)
    to_scalar.wait()

    lane = iota((PPD, 128), 1)
    odd = lax.rem(lax.div(lane, 32), 2) == 1
    low = iota((PPD // 2, 128), 1) < 64

    def correlate(j, carry):
        number = peer(j)
        for k in range(PPD):
            first = jnp.clip(place_ref[number, 0, k], 0, TOTAL - 1)
            second = jnp.clip(place_ref[number, 0, PPD + k], 0, TOTAL - 1)
            first_ref[k : k + 1, :] = wide_ref[pl.ds(first, 1), :]
            second_ref[k : k + 1, :] = wide_ref[pl.ds(second, 1), :]
        a, b = first_ref[...], second_ref[...]
        turned = jnp.where(odd, pltpu.roll(b, 32, 1), -pltpu.roll(b, 96, 1))
        real, imag = a * b, a * turned
        real = real + pltpu.roll(real, 64, 1)
        real = real + pltpu.roll(real, 32, 1)
        imag = imag + pltpu.roll(imag, 64, 1)
        imag = imag + pltpu.roll(imag, 32, 1)
        both = jnp.where(odd, imag, real)
        packed = jnp.where(low, both[: PPD // 2], both[PPD // 2 :])
        cross_ref[number] = packed.astype(BF16).reshape(3, 8, 128)

        @pl.when(j > 1)
        def _():
            cross_copy(peer(j - 1), me).start()

        return carry

    lax.fori_loop(1, LAYER + 1, correlate, 0)
    got_ref[me] = cross_ref[me]

    def cross_arrival(j, carry):
        number = peer(j)
        cross_copy(number, number).wait_recv()
        return carry

    lax.fori_loop(1, LAYER, cross_arrival, 0)

    for i in range(LAYER // 2):
        one = got_ref[2 * i].astype(F32).reshape(PPD // 2, 128)
        two = got_ref[2 * i + 1].astype(F32).reshape(PPD // 2, 128)
        top = jnp.where(low, one, pltpu.roll(two, 64, 1))
        bottom = jnp.where(low, pltpu.roll(one, 64, 1), two)
        left_ref[:, 128 * i : 128 * i + 128] = jnp.concatenate([top, bottom], axis=0).astype(BF16)

    scale = 1.0 / math.sqrt(HALF * W)

    def product(n, carry):
        cols = pl.ds(pl.multiple_of(256 * n, 256), 256)
        out_ref[:, cols] = jnp.dot(left_ref[...], table_ref[:, cols], preferred_element_type=F32) * scale
        return carry

    lax.fori_loop(0, 7, product, 0)
    tail = jnp.dot(left_ref[...], table_ref[:, 1792:2048], preferred_element_type=F32) * scale
    out_ref[:, 1792:LAGS] = tail[:, : LAGS - 1792]

    def sent(j, carry):
        number = peer(j)
        piece_copy(number).wait_send()
        index_copy(number, me).wait_send()
        cross_copy(number, me).wait_send()
        return carry

    lax.fori_loop(1, LAYER, sent, 0)

    def ring_sent(d, carry):
        for s in range(NX):
            for way in range(2):
                ring_copy(way, d, s, z).wait_send()
        return carry

    lax.fori_loop(0, 7, ring_sent, 0)
    for k in range(NX):
        s = lax.rem(x + k, NX)
        ring_copy(0 if k < 2 else 1, 7, s, z).wait_send()


def on_device(spectra, row_station, row_window, station_owner, tile_stations, pair_index):
    vmem = pl.BlockSpec(memory_space=pltpu.VMEM)
    dma = pltpu.SemaphoreType.DMA
    result = pl.pallas_call(
        kernel,
        out_shape=jax.ShapeDtypeStruct((PPD, LAGS), F32),
        in_specs=[vmem] * 6,
        out_specs=vmem,
        scratch_shapes=[
            pltpu.VMEM((LAYER, STA, 128), BF16),
            pltpu.VMEM((NZ, LAYER, STA, 128), BF16),
            pltpu.VMEM((TOTAL, 128), F32),
            pltpu.VMEM((LAYER, 1, 128), I32),
            pltpu.SMEM((LAYER, 1, 128), I32),
            pltpu.VMEM((PPD, 128), F32),
            pltpu.VMEM((PPD, 128), F32),
            pltpu.VMEM((LAYER, 3, 8, 128), BF16),
            pltpu.VMEM((LAYER, 3, 8, 128), BF16),
            pltpu.VMEM((PPD, NFFT), BF16),
            pltpu.VMEM((NFFT, NFFT), BF16),
            pltpu.VMEM((128, 128), F32),
            pltpu.VMEM((128, 128), F32),
            pltpu.VMEM((16, 8, 128), F32),
            pltpu.VMEM((16, 8, 128), F32),
            dma((LAYER,)),
            dma((LAYER,)),
            dma((LAYER,)),
            dma((LAYER,)),
            dma((LAYER,)),
            dma((LAYER,)),
            dma((2, 8, NX)),
            dma((2, 8, NX)),
            dma,
        ],
        compiler_params=pltpu.CompilerParams(
            collective_id=0, has_side_effects=True, vmem_limit_bytes=48 * 1024 * 1024
        ),
    )(
        spectra.reshape(2 * STA, NFFT),
        row_station.reshape(1, 2 * STA),
        row_window.reshape(1, 2 * STA),
        station_owner.reshape(32, 128),
        tile_stations,
        pair_index.reshape(2, PPD),
    )
    return result.reshape(1, 1, PPD, LAGS)


def solution(mesh):
    placed = (
        P(("pairs", "grp"), None, None),
        P(("pairs", "grp")),
        P(("pairs", "grp")),
        P(),
        P(),
        P("pairs", "grp", None, None),
    )
    return jax.shard_map(
        on_device,
        mesh=mesh,
        in_specs=placed,
        out_specs=P("pairs", "grp", None, None),
        check_vma=False,
    )
```

time: 107 us -> 68.8 us (0.64)
  Pallas kernels: 0 us -> 64.7 us
  starting transfers between devices: 36.9 us -> 0 us
  other arithmetic: 30.2 us -> 0 us
  local copies, waits for them, and re-layouts: 31.9 us -> 3.89 us
  matrix products: 6.81 us -> 0 us
    pallas_call x0 -> x1, Pallas kernels: none -> 64.7 us  [on_device(): pl.pallas_call(kernel, out_shape=jax.ShapeDtypeStruct((PPD, LAGS), F32),...]
    all_to_all x3 -> x0, starting transfers between devices: 36.9 us -> none  [the longest x1 19 us: on_device(): lax.all_to_all(outgoing, ('pairs', 'grp'), split_axis=0, concat_axis=0, t...]
    another operation x2 -> x0, other arithmetic: 17.5 us -> none
    gather x5 -> x0, local copies, waits for them, and re-layouts: 12.5 us -> none  [the longest x1 2.8 us: on_device(): owner[pairs[:, 0].reshape(-1)]]
    neg x1 -> x0, local copies, waits for them, and re-layouts: 7.32 us -> none  [lag_table(): imag = -(sa * cb + ca * sb).reshape(HALF, 2048)]
    sub x1 -> x0, local copies, waits for them, and re-layouts: 7.3 us -> none  [lag_table(): real = (ca * cb - sa * sb).reshape(HALF, 2048)]
    dot_general x2 -> x0, matrix products: 6.81 us -> none  [the longest x1 5.7 us: on_device(): jnp.dot(cross, lag_table(), preferred_element_type=jnp.float32)[:, :LAGS]]
    sin x2 -> x0, other arithmetic: 4.12 us -> none  [the longest x1 2.06 us: lag_table(): jnp.sin(a)]
  transfers between devices with their start and end apart: 3 -> 0, of which waited for: 0 -> 0; matrix products, arithmetic and copies ran while one was open for 50% -> 0% of each run, Pallas kernels for 0% -> 0%
where the time goes in v2:
time: 68.8 us; the launch traced here: 68.6 us
  Pallas kernels  64.7 us (94%)
  local copies, waits for them, and re-layouts  3.89 us (6%)
    pallas_call x1, Pallas kernels, on_device(): pl.pallas_call(kernel, out_shape=jax.ShapeDtypeStruct((PPD, LAGS), F32),...  64.7 us
    unnamed x13, local copies, waits for them, and re-layouts  3.89 us

profile of v2, /device:TPU:1, one launch (start us, length us, event | category | flops | bytes accessed | tf_op | source)
XLA Modules:
  0.0 68.6 jit_solution(10830617271588668980)
XLA Ops:
  0.0 0.0 copy-start.5
  0.0 0.0 copy-start.3
  0.0 0.0 copy-start.4
  0.0 0.6 copy-done.5
  0.7 0.0 copy-done.3
  0.7 0.0 copy-done.4
  0.7 0.0 copy-start
  0.7 0.9 %copy-done = s32[64,384]{1,0:T(8,128)S(1)} copy-done((s32[64,384]{1,0:T(8,128)S(1)}, s32[64,384]{1,0:T(8,128)}, u32[]{:S(2)}) %copy-start) | copy-done | bytes 98328
  1.6 0.0 copy-start.1
  1.6 0.8 %copy-done.1 = bf16[16,1,2048]{2,0,1:T(8,128)(2,1)S(1)} copy-done((bf16[16,1,2048]{2,0,1:T(8,128)(2,1)S(1)}, bf16[16,1,2048]{2,0,1:T(8,128)(2,1)}, u32[]{:S(2)}) %copy-start.1) | copy-done | bytes 65560
  2.4 0.0 copy-start.2
  2.4 0.7 %copy-done.2 = s32[4096]{0:T(1024)S(1)} copy-done((s32[4096]{0:T(1024)S(1)}, s32[4096]{0:T(1024)}, u32[]{:S(2)}) %copy-start.2) | copy-done | bytes 16408
  3.1 64.7 %shard_map.64 = f32[48,2001]{1,0:T(8,128)S(1)} custom-call(bf16[16,2048]{1,0:T(8,128)(2,1)S(1)} %bitcast.7, s32[1,16]{1,0:T(1,128)S(1)} %bitcast.10, s32[1,16]{1,0:T(1,128)S(1)} %bitcast.11, s32[32,128]{1,0:T(8,128)S(1)} %bitcast.8, s32[64,384]{1,0:T(8,128)S(1)} %copy-done, s32[2,48]{1,0:T(2,128)S(1)} %bitcast.9), custom_call_target="tpu_custom_call" | custom-call | tf_op jit(solution)/shard_map/pallas_call | solution.py:354
  67.8 0.7 %copy.8 = f32[1,1,48,2001]{3,2,1,0:T(8,128)} copy(f32[1,1,48,2001]{3,2,1,0:T(8,128)S(1)} %bitcast.6) | data formatting | bytes 768384
Async XLA Ops:
  0.0 0.7 copy-start.5
  0.0 0.7 %copy-start.3 = (s32[1,1,2,48]{3,2,1,0:T(2,128)S(1)}, s32[1,1,2,48]{3,2,1,0:T(2,128)}, u32[]{:S(2)}) copy-start(s32[1,1,2,48]{3,2,1,0:T(2,128)} %param.11) | copy-start | bytes 1156
  0.0 0.7 %copy-start.4 = (s32[16]{0:T(128)S(1)}, s32[16]{0:T(128)}, u32[]{:S(2)}) copy-start(s32[16]{0:T(128)} %param.7) | copy-start | bytes 196
  0.7 0.9 %copy-start = (s32[64,384]{1,0:T(8,128)S(1)}, s32[64,384]{1,0:T(8,128)}, u32[]{:S(2)}) copy-start(s32[64,384]{1,0:T(8,128)} %tiles_ref.1) | copy-start | bytes 294916
  1.6 0.8 %copy-start.1 = (bf16[16,1,2048]{2,0,1:T(8,128)(2,1)S(1)}, bf16[16,1,2048]{2,0,1:T(8,128)(2,1)}, u32[]{:S(2)}) copy-start(bf16[16,1,2048]{2,0,1:T(8,128)(2,1)} %param.6) | copy-start | bytes 196612
  2.4 0.7 %copy-start.2 = (s32[4096]{0:T(1024)S(1)}, s32[4096]{0:T(1024)}, u32[]{:S(2)}) copy-start(s32[4096]{0:T(1024)} %param.9) | copy-start | bytes 49156

commit v3 on v2

--- a/solution.py
+++ b/solution.py
@@ -21,6 +21,8 @@
 STA = 8
 PPD = 48
 TOTAL = NZ * LAYER * STA
+HALVES = 2
+PART = LAYER // HALVES
 STEP = 2.0 * math.pi / NFFT
 F32 = jnp.float32
 I32 = jnp.int32
@@ -89,11 +91,12 @@
     return jnp.sum(spread, axis=0, keepdims=True)
 
 
-def build_table(table_ref, c8_ref, s8_ref, dc_ref, ds_ref):
+def table_angles(c8_ref, s8_ref, dc_ref, ds_ref, base_ref):
     shift = NFFT - MAXLAG
     sub, lane = iota((8, 128), 0), iota((8, 128), 1)
     fine = angle(sub * (lane + shift))
-    c0, s0 = jnp.cos(fine), jnp.sin(fine)
+    base_ref[0] = jnp.cos(fine)
+    base_ref[1] = jnp.sin(fine)
     coarse = angle(8 * iota((128, 128), 0) * (iota((128, 128), 1) + shift))
     c8_ref[...] = jnp.cos(coarse)
     s8_ref[...] = jnp.sin(coarse)
@@ -102,7 +105,10 @@
         dc_ref[j] = jnp.cos(turn)
         ds_ref[j] = jnp.sin(turn)
 
+
+def build_table(start, stop, table_ref, c8_ref, s8_ref, dc_ref, ds_ref, base_ref):
     def block(u, carry):
+        c0, s0 = base_ref[0], base_ref[1]
         for h in range(2):
             base = []
             for q in range(2):
@@ -126,40 +132,53 @@
                 table_ref[pl.ds(low, 16), cols] = jnp.concatenate(imags, axis=0).astype(BF16)
         return carry
 
-    lax.fori_loop(0, LAYER, block, 0)
+    lax.fori_loop(start, stop, block, 0)
 
 
 def kernel(
-    spec_ref, station_ref, window_ref, owner_ref, tiles_ref, pair_ref, out_ref,
+    spec_hbm, station_hbm, window_hbm, owner_hbm, tiles_hbm, pair_hbm, out_ref,
+    spec_ref, station_ref, window_ref, owner_ref, tiles_ref, pair_ref,
     send_ref, rows_ref, wide_ref, index_ref, place_ref, first_ref, second_ref, cross_ref, got_ref, left_ref,
-    table_ref, c8_ref, s8_ref, dc_ref, ds_ref,
-    piece_send, piece_recv, index_send, index_recv, cross_send, cross_recv, ring_send, ring_recv, local_sem,
+    table_ref, c8_ref, s8_ref, dc_ref, ds_ref, base_ref,
+    piece_send, piece_recv, index_send, index_recv, cross_send, cross_recv, ring_send, ring_recv, load_sem, local_sem,
 ):
     group, member = lax.axis_index("pairs"), lax.axis_index("grp")
     x, z = lax.div(group, NZ), lax.rem(group, NZ)
     me = x * NG + member
+    sources = (spec_hbm, station_hbm, window_hbm, owner_hbm, tiles_hbm, pair_hbm)
+    targets = (spec_ref, station_ref, window_ref, owner_ref, tiles_ref, pair_ref)
+    loads = [pltpu.make_async_copy(a, b, load_sem.at[n]) for n, (a, b) in enumerate(zip(sources, targets))]
+    for load in loads:
+        load.start()
 
     def device(number, layer):
         return (lax.div(number, NG) * NZ + layer, lax.rem(number, NG))
 
     def peer(j):
-        return lax.rem(me + j, LAYER)
-
-    ahead, behind = lax.rem(z + 1, NZ), lax.rem(z + NZ - 1, NZ)
+        t = lax.div(j, NG)
+        along = jnp.where(t == 0, 2, jnp.where(t == 1, 1, jnp.where(t == 2, 3, 0)))
+        return lax.rem(x + along, NX) * NG + lax.rem(member + 2 * NG - 1 - lax.rem(j, NG), NG)
+
+    def layer_at(offset):
+        return lax.rem(z + NZ + offset, NZ)
+
     barrier = pltpu.get_barrier_semaphore()
 
     def greet(j, carry):
         pl.semaphore_signal(barrier, inc=1, device_id=device(peer(j), z), device_id_type=MESH)
         return carry
 
-    lax.fori_loop(1, LAYER, greet, 0)
-    pl.semaphore_signal(barrier, inc=1, device_id=device(me, ahead), device_id_type=MESH)
-    pl.semaphore_signal(barrier, inc=1, device_id=device(me, behind), device_id_type=MESH)
-
+    for offset in (2, -2, 1, -1):
+        pl.semaphore_signal(barrier, inc=1, device_id=device(me, layer_at(offset)), device_id_type=MESH)
+    lax.fori_loop(0, LAYER - 1, greet, 0)
+
+    for load in loads[:3]:
+        load.wait()
     pack_rows(spec_ref, station_ref, window_ref, send_ref)
-    index_ref[me] = locate(pair_ref, tiles_ref, owner_ref, group)
     rows_ref[z, me] = send_ref[me]
-    pl.semaphore_wait(barrier, LAYER + 1)
+    for load in loads[3:]:
+        load.wait()
+    pl.semaphore_wait(barrier, LAYER - 1 + 4)
 
     def piece_copy(number):
         return pltpu.make_async_remote_copy(
@@ -193,82 +212,114 @@
         piece_copy(peer(j)).start()
         return carry
 
-    lax.fori_loop(1, LAYER, send_pieces, 0)
+    lax.fori_loop(0, LAYER - 1, send_pieces, 0)
+    index_ref[me] = locate(pair_ref, tiles_ref, owner_ref, group)
+    table_angles(c8_ref, s8_ref, dc_ref, ds_ref, base_ref)
 
     def send_index(j, carry):
         index_copy(peer(j), me).start()
         return carry
 
-    lax.fori_loop(1, LAYER, send_index, 0)
-
-    build_table(table_ref, c8_ref, s8_ref, dc_ref, ds_ref)
-
-    def ring_copy(way, d, s, chunk):
-        part = pl.ds(NG * s, NG)
+    lax.fori_loop(0, LAYER - 1, send_index, 0)
+
+    def table_part(start, stop):
+        build_table(start, stop, table_ref, c8_ref, s8_ref, dc_ref, ds_ref, base_ref)
+
+    def ring_copy(way, distance, s, chunk, step):
+        part = pl.ds(PART * s, PART)
         return pltpu.make_async_remote_copy(
             src_ref=rows_ref.at[chunk, part], dst_ref=rows_ref.at[chunk, part],
-            send_sem=ring_send.at[way, d, s], recv_sem=ring_recv.at[way, d, s],
-            device_id=device(me, ahead if way == 0 else behind), device_id_type=MESH,
+            send_sem=ring_send.at[way, distance, s], recv_sem=ring_recv.at[way, distance, s],
+            device_id=device(me, layer_at(step if way == 0 else -step)), device_id_type=MESH,
         )
 
     def widen(chunk, s):
-        start = pl.multiple_of((chunk * LAYER + s * NG) * STA, 64)
-        wide_ref[pl.ds(start, NG * STA), :] = rows_ref[chunk, pl.ds(NG * s, NG)].astype(F32).reshape(NG * STA, 128)
-
-    def chunk_of(way, d):
-        return lax.rem(z + NZ - d, NZ) if way == 0 else lax.rem(z + d, NZ)
-
-    for k in range(NX):
-        s = lax.rem(x + k, NX)
-
-        def arrival(m, carry):
-            number = s * NG + m
+        start = pl.multiple_of((chunk * LAYER + s * PART) * STA, 128)
+        rows = rows_ref[chunk, pl.ds(PART * s, PART)].astype(F32)
+        wide_ref[pl.ds(start, PART * STA), :] = rows.reshape(PART * STA, 128)
+
+    def chunk_of(way, distance):
+        return lax.rem(z + NZ - distance, NZ) if way == 0 else lax.rem(z + distance, NZ)
+
+    def half(k):
+        return lax.rem(lax.div(x, 2) + k, HALVES)
+
+    def start_half(k, carry):
+        s = half(k)
+
+        def arrival(m, c):
+            number = s * PART + m
 
             @pl.when(number != me)
             def _():
                 piece_arrival(number).wait_recv()
 
-            return carry
-
-        lax.fori_loop(0, NG, arrival, 0)
-        ring_copy(0, 0, s, z).start()
-        ring_copy(1, 0, s, z).start()
+            return c
+
+        lax.fori_loop(0, PART, arrival, 0)
+        for way in range(2):
+            ring_copy(way, 2, s, z, 2).start()
+            ring_copy(way, 1, s, z, 1).start()
+        return carry
+
+    lax.fori_loop(0, HALVES, start_half, 0)
+    for s in range(HALVES):
         widen(z, s)
+    table_part(0, 6)
 
     def index_arrival(j, carry):
         number = peer(j)
         index_copy(number, number).wait_recv()
         return carry
 
-    lax.fori_loop(1, LAYER, index_arrival, 0)
+    lax.fori_loop(0, LAYER - 1, index_arrival, 0)
     to_scalar = pltpu.make_async_copy(index_ref, place_ref, local_sem)
     to_scalar.start()
 
-    def hop(d, carry):
-        for k in range(NX):
-            s = lax.rem(x + k, NX)
+    def stop(i, carry):
+        distance = 2 * i + 2
+
+        def one_half(k, c):
+            s = half(k)
             for way in range(2):
-                chunk = chunk_of(way, d + 1)
-                ring_copy(way, d, s, chunk).wait_recv()
-                ring_copy(way, d + 1, s, chunk).start()
+                chunk = chunk_of(way, distance)
+
+                @pl.when((distance < 8) | (k == way))
+                def _():
+                    ring_copy(way, distance, s, chunk, 2).wait_recv()
+
+                @pl.when((distance < 6) | ((distance == 6) & (k == way)))
+                def _():
+                    ring_copy(way, distance + 2, s, chunk, 2).start()
+
+                @pl.when(distance < 8)
+                def _():
+                    ring_copy(way, distance + 1, s, chunk, 1).start()
+
+                @pl.when((distance < 8) | (k == way))
+                def _():
+                    widen(chunk, s)
+            return c
+
+        lax.fori_loop(0, HALVES, one_half, 0)
+
+        def odd_half(k, c):
+            s = half(k)
+            for way in range(2):
+                chunk = chunk_of(way, distance - 1)
+                ring_copy(way, distance - 1, s, chunk, 1).wait_recv()
                 widen(chunk, s)
-        return carry
-
-    lax.fori_loop(0, 6, hop, 0)
-    for k in range(NX):
-        s = lax.rem(x + k, NX)
-        for way in range(2):
-            chunk = chunk_of(way, 7)
-            ring_copy(way, 6, s, chunk).wait_recv()
-            if (k < 2) == (way == 0):
-                ring_copy(way, 7, s, chunk).start()
-            widen(chunk, s)
-    for k in range(NX):
-        s = lax.rem(x + k, NX)
-        way = 0 if k < 2 else 1
-        chunk = chunk_of(way, 8)
-        ring_copy(way, 7, s, chunk).wait_recv()
-        widen(chunk, s)
+            return c
+
+        lax.fori_loop(0, HALVES, odd_half, 0)
+
+        @pl.when(distance < 8)
+        def _():
+            table_part(6 + 9 * i, jnp.minimum(15 + 9 * i, LAYER))
+
+        return carry
+
+    lax.fori_loop(0, 4, stop, 0)
     to_scalar.wait()
 
     lane = iota((PPD, 128), 1)
@@ -278,8 +329,8 @@
     def correlate(j, carry):
         number = peer(j)
         for k in range(PPD):
-            first = jnp.clip(place_ref[number, 0, k], 0, TOTAL - 1)
-            second = jnp.clip(place_ref[number, 0, PPD + k], 0, TOTAL - 1)
+            first = place_ref[number, 0, k] & (TOTAL - 1)
+            second = place_ref[number, 0, PPD + k] & (TOTAL - 1)
             first_ref[k : k + 1, :] = wide_ref[pl.ds(first, 1), :]
             second_ref[k : k + 1, :] = wide_ref[pl.ds(second, 1), :]
         a, b = first_ref[...], second_ref[...]
@@ -293,13 +344,13 @@
         packed = jnp.where(low, both[: PPD // 2], both[PPD // 2 :])
         cross_ref[number] = packed.astype(BF16).reshape(3, 8, 128)
 
-        @pl.when(j > 1)
+        @pl.when(j > 0)
         def _():
             cross_copy(peer(j - 1), me).start()
 
         return carry
 
-    lax.fori_loop(1, LAYER + 1, correlate, 0)
+    lax.fori_loop(0, LAYER, correlate, 0)
     got_ref[me] = cross_ref[me]
 
     def cross_arrival(j, carry):
@@ -307,7 +358,7 @@
         cross_copy(number, number).wait_recv()
         return carry
 
-    lax.fori_loop(1, LAYER, cross_arrival, 0)
+    lax.fori_loop(0, LAYER - 1, cross_arrival, 0)
 
     for i in range(LAYER // 2):
         one = got_ref[2 * i].astype(F32).reshape(PPD // 2, 128)
@@ -334,18 +385,19 @@
         cross_copy(number, me).wait_send()
         return carry
 
-    lax.fori_loop(1, LAYER, sent, 0)
-
-    def ring_sent(d, carry):
-        for s in range(NX):
-            for way in range(2):
-                ring_copy(way, d, s, z).wait_send()
-        return carry
-
-    lax.fori_loop(0, 7, ring_sent, 0)
-    for k in range(NX):
-        s = lax.rem(x + k, NX)
-        ring_copy(0 if k < 2 else 1, 7, s, z).wait_send()
+    lax.fori_loop(0, LAYER - 1, sent, 0)
+
+    def ring_sent(i, carry):
+        distance, k = lax.div(i, HALVES) + 1, lax.rem(i, HALVES)
+        for way in range(2):
+
+            @pl.when((distance < 8) | (k == way))
+            def _():
+                ring_copy(way, distance, half(k), z, 1).wait_send()
+
+        return carry
+
+    lax.fori_loop(0, 8 * HALVES, ring_sent, 0)
 
 
 def on_device(spectra, row_station, row_window, station_owner, tile_stations, pair_index):
@@ -354,9 +406,15 @@
     result = pl.pallas_call(
         kernel,
         out_shape=jax.ShapeDtypeStruct((PPD, LAGS), F32),
-        in_specs=[vmem] * 6,
+        in_specs=[pl.BlockSpec(memory_space=pl.ANY)] * 6,
         out_specs=vmem,
         scratch_shapes=[
+            pltpu.VMEM((2 * STA, NFFT), BF16),
+            pltpu.VMEM((1, 2 * STA), I32),
+            pltpu.VMEM((1, 2 * STA), I32),
+            pltpu.VMEM((32, 128), I32),
+            pltpu.VMEM((NX * NZ, NG * PPD), I32),
+            pltpu.VMEM((2, PPD), I32),
             pltpu.VMEM((LAYER, STA, 128), BF16),
             pltpu.VMEM((NZ, LAYER, STA, 128), BF16),
             pltpu.VMEM((TOTAL, 128), F32),
@@ -372,18 +430,20 @@
             pltpu.VMEM((128, 128), F32),
             pltpu.VMEM((16, 8, 128), F32),
             pltpu.VMEM((16, 8, 128), F32),
-            dma((LAYER,)),
-            dma((LAYER,)),
-            dma((LAYER,)),
-            dma((LAYER,)),
-            dma((LAYER,)),
-            dma((LAYER,)),
-            dma((2, 8, NX)),
-            dma((2, 8, NX)),
+            pltpu.VMEM((2, 8, 128), F32),
+            dma((LAYER,)),
+            dma((LAYER,)),
+            dma((LAYER,)),
+            dma((LAYER,)),
+            dma((LAYER,)),
+            dma((LAYER,)),
+            dma((2, 9, HALVES)),
+            dma((2, 9, HALVES)),
+            dma((6,)),
             dma,
         ],
         compiler_params=pltpu.CompilerParams(
-            collective_id=0, has_side_effects=True, vmem_limit_bytes=48 * 1024 * 1024
+            collective_id=0, has_side_effects=True, vmem_limit_bytes=62 * 1024 * 1024
         ),
     )(
         spectra.reshape(2 * STA, NFFT),

time: 68.8 us -> 59.4 us (0.86)
  Pallas kernels: 64.7 us -> 57.4 us
  local copies, waits for them, and re-layouts: 3.89 us -> 1.77 us
    pallas_call x1, Pallas kernels: 64.7 us -> 57.4 us  [on_device(): pl.pallas_call(kernel, out_shape=jax.ShapeDtypeStruct((PPD, LAGS), F32),...]
    unnamed x13 -> x1, local copies, waits for them, and re-layouts: 3.89 us -> 1.77 us
where the time goes in v3:
time: 59.4 us; the launch traced here: 59.2 us
  Pallas kernels  57.4 us (97%)
  local copies, waits for them, and re-layouts  1.77 us (3%)
    pallas_call x1, Pallas kernels, on_device(): pl.pallas_call(kernel, out_shape=jax.ShapeDtypeStruct((PPD, LAGS), F32),...  57.4 us
    unnamed x1, local copies, waits for them, and re-layouts  1.77 us

profile of v3, /device:TPU:1, one launch (start us, length us, event | category | flops | bytes accessed | tf_op | source)
XLA Modules:
  0.0 59.2 jit_solution(16952821533485718254)
XLA Ops:
  0.0 57.4 %shard_map.64 = f32[48,2001]{1,0:T(8,128)} custom-call(bf16[16,2048]{1,0:T(8,128)(2,1)} %bitcast.7, s32[1,16]{1,0:T(1,128)} %bitcast.10, s32[1,16]{1,0:T(1,128)} %bitcast.11, s32[32,128]{1,0:T(8,128)} %bitcast.8, s32[64,384]{1,0:T(8,128)} %tiles_hbm.1, s32[2,48]{1,0:T(2,128)} %bitcast.9), custom_call_target="tpu_custom_call" | custom-call | tf_op jit(solution)/shard_map/pallas_call | solution.py:406
  57.5 1.8 %copy.8 = f32[1,1,48,2001]{3,2,1,0:T(8,128)} copy(f32[1,1,48,2001]{3,2,1,0:T(8,128)} %bitcast.6) | data formatting | bytes 768384

commit v4 on v3

--- a/solution.py
+++ b/solution.py
@@ -138,7 +138,7 @@
 def kernel(
     spec_hbm, station_hbm, window_hbm, owner_hbm, tiles_hbm, pair_hbm, out_ref,
     spec_ref, station_ref, window_ref, owner_ref, tiles_ref, pair_ref,
-    send_ref, rows_ref, wide_ref, index_ref, place_ref, first_ref, second_ref, cross_ref, got_ref, left_ref,
+    send_ref, rows_ref, wide_ref, index_ref, place_ref, first_ref, second_ref, cross_ref, got_ref, left_ref, total_ref,
     table_ref, c8_ref, s8_ref, dc_ref, ds_ref, base_ref,
     piece_send, piece_recv, index_send, index_recv, cross_send, cross_recv, ring_send, ring_recv, load_sem, local_sem,
 ):
@@ -151,26 +151,47 @@
     for load in loads:
         load.start()
 
-    def device(number, layer):
-        return (lax.div(number, NG) * NZ + layer, lax.rem(number, NG))
-
-    def peer(j):
-        t = lax.div(j, NG)
-        along = jnp.where(t == 0, 2, jnp.where(t == 1, 1, jnp.where(t == 2, 3, 0)))
-        return lax.rem(x + along, NX) * NG + lax.rem(member + 2 * NG - 1 - lax.rem(j, NG), NG)
+    def device(along, across, layer):
+        return (along * NZ + layer, across)
+
+    def column(t):
+        return lax.rem(x + jnp.where(t == 0, 2, jnp.where(t == 1, 1, jnp.where(t == 2, 3, 0))), NX)
+
+    def across(m):
+        return lax.rem(member + 2 * NG - 1 - m, NG)
+
+    def each_peer(act):
+        def one_column(t, carry):
+            along = column(t)
+
+            def one(m, c):
+                act(along, across(m))
+                return c
+
+            return lax.fori_loop(0, jnp.where(t < NX - 1, NG, NG - 1), one, carry)
+
+        lax.fori_loop(0, NX, one_column, 0)
 
     def layer_at(offset):
         return lax.rem(z + NZ + offset, NZ)
 
+    def arrived(ref, sem):
+        pltpu.make_async_remote_copy(
+            src_ref=ref, dst_ref=ref, send_sem=piece_send, recv_sem=sem,
+            device_id=device(x, member, layer_at(1)), device_id_type=MESH,
+        ).wait_recv()
+
+    def left(ref, sem):
+        pltpu.make_async_remote_copy(
+            src_ref=ref, dst_ref=ref, send_sem=sem, recv_sem=index_recv,
+            device_id=device(x, member, layer_at(1)), device_id_type=MESH,
+        ).wait_send()
+
     barrier = pltpu.get_barrier_semaphore()
 
-    def greet(j, carry):
-        pl.semaphore_signal(barrier, inc=1, device_id=device(peer(j), z), device_id_type=MESH)
-        return carry
-
     for offset in (2, -2, 1, -1):
-        pl.semaphore_signal(barrier, inc=1, device_id=device(me, layer_at(offset)), device_id_type=MESH)
-    lax.fori_loop(0, LAYER - 1, greet, 0)
+        pl.semaphore_signal(barrier, inc=1, device_id=device(x, member, layer_at(offset)), device_id_type=MESH)
+    each_peer(lambda a, m: pl.semaphore_signal(barrier, inc=1, device_id=device(a, m, z), device_id_type=MESH))
 
     for load in loads[:3]:
         load.wait()
@@ -180,47 +201,31 @@
         load.wait()
     pl.semaphore_wait(barrier, LAYER - 1 + 4)
 
-    def piece_copy(number):
+    def piece_copy(along, across):
         return pltpu.make_async_remote_copy(
-            src_ref=send_ref.at[number], dst_ref=rows_ref.at[z, me],
-            send_sem=piece_send.at[number], recv_sem=piece_recv.at[me],
-            device_id=device(number, z), device_id_type=MESH,
+            src_ref=send_ref.at[along * NG + across], dst_ref=rows_ref.at[z, me],
+            send_sem=piece_send, recv_sem=piece_recv.at[lax.div(x, NX // HALVES)],
+            device_id=device(along, across, z), device_id_type=MESH,
         )
 
-    def piece_arrival(number):
+    def index_copy(along, across):
         return pltpu.make_async_remote_copy(
-            src_ref=send_ref.at[number], dst_ref=rows_ref.at[z, number],
-            send_sem=piece_send.at[number], recv_sem=piece_recv.at[number],
-            device_id=device(number, z), device_id_type=MESH,
+            src_ref=index_ref.at[me], dst_ref=index_ref.at[me],
+            send_sem=index_send, recv_sem=index_recv,
+            device_id=device(along, across, z), device_id_type=MESH,
         )
 
-    def index_copy(number, source):
+    def cross_copy(along, across):
         return pltpu.make_async_remote_copy(
-            src_ref=index_ref.at[me], dst_ref=index_ref.at[source],
-            send_sem=index_send.at[number], recv_sem=index_recv.at[source],
-            device_id=device(number, z), device_id_type=MESH,
+            src_ref=cross_ref.at[along * NG + across], dst_ref=got_ref.at[me],
+            send_sem=cross_send, recv_sem=cross_recv.at[x],
+            device_id=device(along, across, z), device_id_type=MESH,
         )
 
-    def cross_copy(number, source):
-        return pltpu.make_async_remote_copy(
-            src_ref=cross_ref.at[number], dst_ref=got_ref.at[source],
-            send_sem=cross_send.at[number], recv_sem=cross_recv.at[source],
-            device_id=device(number, z), device_id_type=MESH,
-        )
-
-    def send_pieces(j, carry):
-        piece_copy(peer(j)).start()
-        return carry
-
-    lax.fori_loop(0, LAYER - 1, send_pieces, 0)
+    each_peer(lambda a, m: piece_copy(a, m).start())
     index_ref[me] = locate(pair_ref, tiles_ref, owner_ref, group)
     table_angles(c8_ref, s8_ref, dc_ref, ds_ref, base_ref)
-
-    def send_index(j, carry):
-        index_copy(peer(j), me).start()
-        return carry
-
-    lax.fori_loop(0, LAYER - 1, send_index, 0)
+    each_peer(lambda a, m: index_copy(a, m).start())
 
     def table_part(start, stop):
         build_table(start, stop, table_ref, c8_ref, s8_ref, dc_ref, ds_ref, base_ref)
@@ -229,8 +234,8 @@
         part = pl.ds(PART * s, PART)
         return pltpu.make_async_remote_copy(
             src_ref=rows_ref.at[chunk, part], dst_ref=rows_ref.at[chunk, part],
-            send_sem=ring_send.at[way, distance, s], recv_sem=ring_recv.at[way, distance, s],
-            device_id=device(me, layer_at(step if way == 0 else -step)), device_id_type=MESH,
+            send_sem=ring_send, recv_sem=ring_recv.at[way, distance, s],
+            device_id=device(x, member, layer_at(step if way == 0 else -step)), device_id_type=MESH,
         )
 
     def widen(chunk, s):
@@ -247,16 +252,14 @@
     def start_half(k, carry):
         s = half(k)
 
-        def arrival(m, c):
-            number = s * PART + m
-
-            @pl.when(number != me)
-            def _():
-                piece_arrival(number).wait_recv()
-
-            return c
-
-        lax.fori_loop(0, PART, arrival, 0)
+        @pl.when(k == 0)
+        def _():
+            arrived(rows_ref.at[z, pl.ds(PART * s, PART - 1)], piece_recv.at[s])
+
+        @pl.when(k == 1)
+        def _():
+            arrived(rows_ref.at[z, pl.ds(PART * s, PART)], piece_recv.at[s])
+
         for way in range(2):
             ring_copy(way, 2, s, z, 2).start()
             ring_copy(way, 1, s, z, 1).start()
@@ -267,12 +270,7 @@
         widen(z, s)
     table_part(0, 6)
 
-    def index_arrival(j, carry):
-        number = peer(j)
-        index_copy(number, number).wait_recv()
-        return carry
-
-    lax.fori_loop(0, LAYER - 1, index_arrival, 0)
+    arrived(index_ref.at[pl.ds(0, LAYER - 1)], index_recv)
     to_scalar = pltpu.make_async_copy(index_ref, place_ref, local_sem)
     to_scalar.start()
 
@@ -326,14 +324,20 @@
     odd = lax.rem(lax.div(lane, 32), 2) == 1
     low = iota((PPD // 2, 128), 1) < 64
 
+    first_ref[...] = jnp.zeros((PPD, 128), F32)
+    second_ref[...] = jnp.zeros((PPD, 128), F32)
+
     def correlate(j, carry):
-        number = peer(j)
+        a, b = first_ref[...], second_ref[...]
+        last_a, last_m, before_a, before_m = carry
+        turn = jnp.minimum(j, LAYER - 1)
+        now_a, now_m = column(lax.div(turn, NG)), across(lax.rem(turn, NG))
+        number = now_a * NG + now_m
         for k in range(PPD):
             first = place_ref[number, 0, k] & (TOTAL - 1)
             second = place_ref[number, 0, PPD + k] & (TOTAL - 1)
             first_ref[k : k + 1, :] = wide_ref[pl.ds(first, 1), :]
             second_ref[k : k + 1, :] = wide_ref[pl.ds(second, 1), :]
-        a, b = first_ref[...], second_ref[...]
         turned = jnp.where(odd, pltpu.roll(b, 32, 1), -pltpu.roll(b, 96, 1))
         real, imag = a * b, a * turned
         real = real + pltpu.roll(real, 64, 1)
@@ -342,62 +346,57 @@
         imag = imag + pltpu.roll(imag, 32, 1)
         both = jnp.where(odd, imag, real)
         packed = jnp.where(low, both[: PPD // 2], both[PPD // 2 :])
-        cross_ref[number] = packed.astype(BF16).reshape(3, 8, 128)
-
-        @pl.when(j > 0)
-        def _():
-            cross_copy(peer(j - 1), me).start()
-
+        cross_ref[last_a * NG + last_m] = packed.astype(BF16).reshape(3, 8, 128)
+
+        @pl.when(j > 1)
+        def _():
+            cross_copy(before_a, before_m).start()
+
+        return now_a, now_m, last_a, last_m
+
+    start = (column(0), across(0), column(0), across(0))
+    lax.fori_loop(0, LAYER + 1, correlate, start)
+    got_ref[me] = cross_ref[me]
+
+    scale = 1.0 / math.sqrt(HALF * W)
+    depth = 2 * HALF // NX
+
+    def product(t, carry):
+        along = column(t)
+        base = along * NG
+
+        @pl.when(t < NX - 1)
+        def _():
+            arrived(got_ref.at[pl.ds(base, NG)], cross_recv.at[along])
+
+        @pl.when(t == NX - 1)
+        def _():
+            arrived(got_ref.at[pl.ds(base, NG - 1)], cross_recv.at[along])
+
+        for i in range(NG // 2):
+            one = got_ref[base + 2 * i].astype(F32).reshape(PPD // 2, 128)
+            two = got_ref[base + 2 * i + 1].astype(F32).reshape(PPD // 2, 128)
+            top = jnp.where(low, one, pltpu.roll(two, 64, 1))
+            bottom = jnp.where(low, pltpu.roll(one, 64, 1), two)
+            left_ref[:, 128 * i : 128 * i + 128] = jnp.concatenate([top, bottom], axis=0).astype(BF16)
+        rows = pl.ds(pl.multiple_of(base * (depth // NG), depth), depth)
+
+        def columns(n, c):
+            cols = pl.ds(pl.multiple_of(256 * n, 256), 256)
+            total_ref[:, cols] += jnp.dot(left_ref[...], table_ref[rows, cols], preferred_element_type=F32)
+            return c
+
+        lax.fori_loop(0, 8, columns, 0)
         return carry
 
-    lax.fori_loop(0, LAYER, correlate, 0)
-    got_ref[me] = cross_ref[me]
-
-    def cross_arrival(j, carry):
-        number = peer(j)
-        cross_copy(number, number).wait_recv()
-        return carry
-
-    lax.fori_loop(0, LAYER - 1, cross_arrival, 0)
-
-    for i in range(LAYER // 2):
-        one = got_ref[2 * i].astype(F32).reshape(PPD // 2, 128)
-        two = got_ref[2 * i + 1].astype(F32).reshape(PPD // 2, 128)
-        top = jnp.where(low, one, pltpu.roll(two, 64, 1))
-        bottom = jnp.where(low, pltpu.roll(one, 64, 1), two)
-        left_ref[:, 128 * i : 128 * i + 128] = jnp.concatenate([top, bottom], axis=0).astype(BF16)
-
-    scale = 1.0 / math.sqrt(HALF * W)
-
-    def product(n, carry):
-        cols = pl.ds(pl.multiple_of(256 * n, 256), 256)
-        out_ref[:, cols] = jnp.dot(left_ref[...], table_ref[:, cols], preferred_element_type=F32) * scale
-        return carry
-
-    lax.fori_loop(0, 7, product, 0)
-    tail = jnp.dot(left_ref[...], table_ref[:, 1792:2048], preferred_element_type=F32) * scale
-    out_ref[:, 1792:LAGS] = tail[:, : LAGS - 1792]
-
-    def sent(j, carry):
-        number = peer(j)
-        piece_copy(number).wait_send()
-        index_copy(number, me).wait_send()
-        cross_copy(number, me).wait_send()
-        return carry
-
-    lax.fori_loop(0, LAYER - 1, sent, 0)
-
-    def ring_sent(i, carry):
-        distance, k = lax.div(i, HALVES) + 1, lax.rem(i, HALVES)
-        for way in range(2):
-
-            @pl.when((distance < 8) | (k == way))
-            def _():
-                ring_copy(way, distance, half(k), z, 1).wait_send()
-
-        return carry
-
-    lax.fori_loop(0, 8 * HALVES, ring_sent, 0)
+    total_ref[...] = jnp.zeros((PPD, NFFT), F32)
+    lax.fori_loop(0, NX, product, 0)
+    out_ref[...] = total_ref[:, :LAGS] * scale
+
+    left(send_ref.at[pl.ds(0, LAYER - 1)], piece_send)
+    left(index_ref.at[pl.ds(0, LAYER - 1)], index_send)
+    left(cross_ref.at[pl.ds(0, LAYER - 1)], cross_send)
+    left(rows_ref.at[pl.ds(0, NZ - 1)], ring_send)
 
 
 def on_device(spectra, row_station, row_window, station_owner, tile_stations, pair_index):
@@ -424,20 +423,21 @@
             pltpu.VMEM((PPD, 128), F32),
             pltpu.VMEM((LAYER, 3, 8, 128), BF16),
             pltpu.VMEM((LAYER, 3, 8, 128), BF16),
-            pltpu.VMEM((PPD, NFFT), BF16),
+            pltpu.VMEM((PPD, NFFT // NX), BF16),
+            pltpu.VMEM((PPD, NFFT), F32),
             pltpu.VMEM((NFFT, NFFT), BF16),
             pltpu.VMEM((128, 128), F32),
             pltpu.VMEM((128, 128), F32),
             pltpu.VMEM((16, 8, 128), F32),
             pltpu.VMEM((16, 8, 128), F32),
             pltpu.VMEM((2, 8, 128), F32),
-            dma((LAYER,)),
-            dma((LAYER,)),
-            dma((LAYER,)),
-            dma((LAYER,)),
-            dma((LAYER,)),
-            dma((LAYER,)),
-            dma((2, 9, HALVES)),
+            dma,
+            dma((HALVES,)),
+            dma,
+            dma,
+            dma,
+            dma((NX,)),
+            dma,
             dma((2, 9, HALVES)),
             dma((6,)),
             dma,

time: 59.4 us -> 55.8 us (0.939)
  Pallas kernels: 57.4 us -> 53.8 us
    pallas_call x1, Pallas kernels: 57.4 us -> 53.8 us  [on_device(): pl.pallas_call(kernel, out_shape=jax.ShapeDtypeStruct((PPD, LAGS), F32),...]
where the time goes in v4:
time: 55.8 us; the launch traced here: 55.6 us
  Pallas kernels  53.8 us (96%)
  local copies, waits for them, and re-layouts  1.77 us (3%)
    pallas_call x1, Pallas kernels, on_device(): pl.pallas_call(kernel, out_shape=jax.ShapeDtypeStruct((PPD, LAGS), F32),...  53.8 us
    unnamed x1, local copies, waits for them, and re-layouts  1.77 us

profile of v4, /device:TPU:1, one launch (start us, length us, event | category | flops | bytes accessed | tf_op | source)
XLA Modules:
  0.0 55.6 jit_solution(13841876971555526780)
XLA Ops:
  0.0 53.8 %shard_map.64 = f32[48,2001]{1,0:T(8,128)} custom-call(bf16[16,2048]{1,0:T(8,128)(2,1)} %bitcast.7, s32[1,16]{1,0:T(1,128)} %bitcast.10, s32[1,16]{1,0:T(1,128)} %bitcast.11, s32[32,128]{1,0:T(8,128)} %bitcast.8, s32[64,384]{1,0:T(8,128)} %tiles_hbm.1, s32[2,48]{1,0:T(2,128)} %bitcast.9), custom_call_target="tpu_custom_call" | custom-call | tf_op jit(solution)/shard_map/pallas_call | solution.py:405
  53.8 1.8 %copy.8 = f32[1,1,48,2001]{3,2,1,0:T(8,128)} copy(f32[1,1,48,2001]{3,2,1,0:T(8,128)} %bitcast.6) | data formatting | bytes 768384

commit v5 on v4

--- a/solution.py
+++ b/solution.py
@@ -56,7 +56,7 @@
         scale = lax.rsqrt(power + EPS)
         real = jnp.dot(order, (real * scale).astype(BF16), preferred_element_type=F32)
         imag = jnp.dot(order, (imag * scale).astype(BF16), preferred_element_type=F32)
-        parts = (real[:STA], imag[:STA], real[STA:], imag[STA:])
+        parts = (real[:STA], real[STA:], imag[:STA], imag[STA:])
         for quarter in range(4):
             piece = None
             for k in range(4):
@@ -323,6 +323,7 @@
     lane = iota((PPD, 128), 1)
     odd = lax.rem(lax.div(lane, 32), 2) == 1
     low = iota((PPD // 2, 128), 1) < 64
+    sign = jnp.where(lane < 64, -1.0, 1.0)
 
     first_ref[...] = jnp.zeros((PPD, 128), F32)
     second_ref[...] = jnp.zeros((PPD, 128), F32)
@@ -338,13 +339,10 @@
             second = place_ref[number, 0, PPD + k] & (TOTAL - 1)
             first_ref[k : k + 1, :] = wide_ref[pl.ds(first, 1), :]
             second_ref[k : k + 1, :] = wide_ref[pl.ds(second, 1), :]
-        turned = jnp.where(odd, pltpu.roll(b, 32, 1), -pltpu.roll(b, 96, 1))
-        real, imag = a * b, a * turned
-        real = real + pltpu.roll(real, 64, 1)
-        real = real + pltpu.roll(real, 32, 1)
-        imag = imag + pltpu.roll(imag, 64, 1)
-        imag = imag + pltpu.roll(imag, 32, 1)
-        both = jnp.where(odd, imag, real)
+        real, imag = a * b, a * (pltpu.roll(b, 64, 1) * sign)
+        kept, moved = jnp.where(odd, imag, real), jnp.where(odd, real, imag)
+        both = kept + pltpu.roll(moved, 96, 1)
+        both = both + pltpu.roll(both, 64, 1)
         packed = jnp.where(low, both[: PPD // 2], both[PPD // 2 :])
         cross_ref[last_a * NG + last_m] = packed.astype(BF16).reshape(3, 8, 128)
 
@@ -405,7 +403,7 @@
     result = pl.pallas_call(
         kernel,
         out_shape=jax.ShapeDtypeStruct((PPD, LAGS), F32),
-        in_specs=[pl.BlockSpec(memory_space=pl.ANY)] * 6,
+        in_specs=[pl.BlockSpec(memory_space=pltpu.HBM)] * 6,
         out_specs=vmem,
         scratch_shapes=[
             pltpu.VMEM((2 * STA, NFFT), BF16),
@@ -443,16 +441,16 @@
             dma,
         ],
         compiler_params=pltpu.CompilerParams(
-            collective_id=0, has_side_effects=True, vmem_limit_bytes=62 * 1024 * 1024
+            collective_id=0, has_side_effects=True, vmem_limit_bytes=48 * 1024 * 1024
         ),
-    )(
+    )(*[pltpu.with_memory_space_constraint(v, pltpu.HBM) for v in (
         spectra.reshape(2 * STA, NFFT),
         row_station.reshape(1, 2 * STA),
         row_window.reshape(1, 2 * STA),
         station_owner.reshape(32, 128),
         tile_stations,
         pair_index.reshape(2, PPD),
-    )
+    )])
     return result.reshape(1, 1, PPD, LAGS)
 
 

time: 55.8 us -> 53.9 us (0.966)
  local copies, waits for them, and re-layouts: 1.77 us -> 0.75 us
  Pallas kernels: 53.8 us -> 53 us
    unnamed x1, local copies, waits for them, and re-layouts: 1.77 us -> 0.75 us
    pallas_call x1, Pallas kernels: 53.8 us -> 53 us  [on_device(): pl.pallas_call(kernel, out_shape=jax.ShapeDtypeStruct((PPD, LAGS), F32),...]
where the time goes in v5:
time: 53.9 us; the launch traced here: 53.8 us
  Pallas kernels  53 us (98%)
  local copies, waits for them, and re-layouts  0.75 us (1%)
    pallas_call x1, Pallas kernels, on_device(): pl.pallas_call(kernel, out_shape=jax.ShapeDtypeStruct((PPD, LAGS), F32),...  53 us

profile of v5, /device:TPU:1, one launch (start us, length us, event | category | flops | bytes accessed | tf_op | source)
XLA Modules:
  0.0 53.8 jit_solution(9378404444610454561)
XLA Ops:
  0.0 53.0 %shard_map.64 = f32[48,2001]{1,0:T(8,128)S(1)} custom-call(bf16[16,2048]{1,0:T(8,128)(2,1)} %bitcast.7, s32[1,16]{1,0:T(1,128)} %bitcast.10, s32[1,16]{1,0:T(1,128)} %bitcast.11, s32[32,128]{1,0:T(8,128)} %bitcast.8, s32[64,384]{1,0:T(8,128)} %tiles_hbm.1, s32[2,48]{1,0:T(2,128)} %bitcast.9), custom_call_target="tpu_custom_call" | custom-call | tf_op jit(solution)/shard_map/pallas_call | solution.py:403
  53.0 0.7 %copy.8 = f32[1,1,48,2001]{3,2,1,0:T(8,128)} copy(f32[1,1,48,2001]{3,2,1,0:T(8,128)S(1)} %bitcast.6) | data formatting | bytes 768384

commit v6 on v5

--- a/solution.py
+++ b/solution.py
@@ -320,41 +320,49 @@
     lax.fori_loop(0, 4, stop, 0)
     to_scalar.wait()
 
-    lane = iota((PPD, 128), 1)
+    lane = iota((2 * PPD, 128), 1)
     odd = lax.rem(lax.div(lane, 32), 2) == 1
     low = iota((PPD // 2, 128), 1) < 64
     sign = jnp.where(lane < 64, -1.0, 1.0)
 
-    first_ref[...] = jnp.zeros((PPD, 128), F32)
-    second_ref[...] = jnp.zeros((PPD, 128), F32)
+    first_ref[...] = jnp.zeros((2 * PPD, 128), F32)
+    second_ref[...] = jnp.zeros((2 * PPD, 128), F32)
 
     def correlate(j, carry):
         a, b = first_ref[...], second_ref[...]
-        last_a, last_m, before_a, before_m = carry
-        turn = jnp.minimum(j, LAYER - 1)
-        now_a, now_m = column(lax.div(turn, NG)), across(lax.rem(turn, NG))
-        number = now_a * NG + now_m
-        for k in range(PPD):
-            first = place_ref[number, 0, k] & (TOTAL - 1)
-            second = place_ref[number, 0, PPD + k] & (TOTAL - 1)
-            first_ref[k : k + 1, :] = wide_ref[pl.ds(first, 1), :]
-            second_ref[k : k + 1, :] = wide_ref[pl.ds(second, 1), :]
+        last, before = carry
+        now = []
+        for i in range(2):
+            turn = jnp.minimum(2 * j, LAYER - 2) + i
+            along, over = column(lax.div(turn, NG)), across(lax.rem(turn, NG))
+            number = along * NG + over
+            now.append((along, over))
+            for k in range(PPD):
+                first = place_ref[number, 0, k] & (TOTAL - 1)
+                second = place_ref[number, 0, PPD + k] & (TOTAL - 1)
+                first_ref[PPD * i + k : PPD * i + k + 1, :] = wide_ref[pl.ds(first, 1), :]
+                second_ref[PPD * i + k : PPD * i + k + 1, :] = wide_ref[pl.ds(second, 1), :]
         real, imag = a * b, a * (pltpu.roll(b, 64, 1) * sign)
         kept, moved = jnp.where(odd, imag, real), jnp.where(odd, real, imag)
         both = kept + pltpu.roll(moved, 96, 1)
         both = both + pltpu.roll(both, 64, 1)
-        packed = jnp.where(low, both[: PPD // 2], both[PPD // 2 :])
-        cross_ref[last_a * NG + last_m] = packed.astype(BF16).reshape(3, 8, 128)
+        for i in range(2):
+            top = both[PPD * i : PPD * i + PPD // 2]
+            packed = jnp.where(low, top, both[PPD * i + PPD // 2 : PPD * i + PPD])
+            cross_ref[last[i][0] * NG + last[i][1]] = packed.astype(BF16).reshape(3, 8, 128)
 
         @pl.when(j > 1)
         def _():
-            cross_copy(before_a, before_m).start()
-
-        return now_a, now_m, last_a, last_m
-
-    start = (column(0), across(0), column(0), across(0))
-    lax.fori_loop(0, LAYER + 1, correlate, start)
+            for i in range(2):
+                cross_copy(*before[i]).start()
+
+        return tuple(now), last
+
+    begin = tuple((column(0), across(i)) for i in range(2))
+    final, _ = lax.fori_loop(0, LAYER // 2 + 1, correlate, (begin, begin))
+    total_ref[...] = jnp.zeros((PPD, NFFT), F32)
     got_ref[me] = cross_ref[me]
+    cross_copy(*final[0]).start()
 
     scale = 1.0 / math.sqrt(HALF * W)
     depth = 2 * HALF // NX
@@ -387,7 +395,6 @@
         lax.fori_loop(0, 8, columns, 0)
         return carry
 
-    total_ref[...] = jnp.zeros((PPD, NFFT), F32)
     lax.fori_loop(0, NX, product, 0)
     out_ref[...] = total_ref[:, :LAGS] * scale
 
@@ -417,8 +424,8 @@
             pltpu.VMEM((TOTAL, 128), F32),
             pltpu.VMEM((LAYER, 1, 128), I32),
             pltpu.SMEM((LAYER, 1, 128), I32),
-            pltpu.VMEM((PPD, 128), F32),
-            pltpu.VMEM((PPD, 128), F32),
+            pltpu.VMEM((2 * PPD, 128), F32),
+            pltpu.VMEM((2 * PPD, 128), F32),
             pltpu.VMEM((LAYER, 3, 8, 128), BF16),
             pltpu.VMEM((LAYER, 3, 8, 128), BF16),
             pltpu.VMEM((PPD, NFFT // NX), BF16),

time: 53.9 us -> 52.4 us (0.972)
  Pallas kernels: 53 us -> 51.5 us
    pallas_call x1, Pallas kernels: 53 us -> 51.5 us  [on_device(): pl.pallas_call(kernel, out_shape=jax.ShapeDtypeStruct((PPD, LAGS), F32),...]
where the time goes in v6:
time: 52.4 us; the launch traced here: 52.3 us
  Pallas kernels  51.5 us (98%)
  local copies, waits for them, and re-layouts  0.75 us (1%)
    pallas_call x1, Pallas kernels, on_device(): pl.pallas_call(kernel, out_shape=jax.ShapeDtypeStruct((PPD, LAGS), F32),...  51.5 us

profile of v6, /device:TPU:1, one launch (start us, length us, event | category | flops | bytes accessed | tf_op | source)
XLA Modules:
  0.0 52.3 jit_solution(4574624654822564568)
XLA Ops:
  0.0 51.5 %shard_map.64 = f32[48,2001]{1,0:T(8,128)S(1)} custom-call(bf16[16,2048]{1,0:T(8,128)(2,1)} %bitcast.7, s32[1,16]{1,0:T(1,128)} %bitcast.10, s32[1,16]{1,0:T(1,128)} %bitcast.11, s32[32,128]{1,0:T(8,128)} %bitcast.8, s32[64,384]{1,0:T(8,128)} %tiles_hbm.1, s32[2,48]{1,0:T(2,128)} %bitcast.9), custom_call_target="tpu_custom_call" | custom-call | tf_op jit(solution)/shard_map/pallas_call | solution.py:410
  51.5 0.7 %copy.8 = f32[1,1,48,2001]{3,2,1,0:T(8,128)} copy(f32[1,1,48,2001]{3,2,1,0:T(8,128)S(1)} %bitcast.6) | data formatting | bytes 768384

commit v7 on v6

--- a/solution.py
+++ b/solution.py
@@ -224,8 +224,8 @@
 
     each_peer(lambda a, m: piece_copy(a, m).start())
     index_ref[me] = locate(pair_ref, tiles_ref, owner_ref, group)
+    each_peer(lambda a, m: index_copy(a, m).start())
     table_angles(c8_ref, s8_ref, dc_ref, ds_ref, base_ref)
-    each_peer(lambda a, m: index_copy(a, m).start())
 
     def table_part(start, stop):
         build_table(start, stop, table_ref, c8_ref, s8_ref, dc_ref, ds_ref, base_ref)

time: 52.4 us -> 52.5 us (level)
  no operation moved by 1% of the time
where the time goes in v7:
time: 52.5 us; the launch traced here: 52.3 us
  Pallas kernels  51.6 us (98%)
  local copies, waits for them, and re-layouts  0.75 us (1%)
    pallas_call x1, Pallas kernels, on_device(): pl.pallas_call(kernel, out_shape=jax.ShapeDtypeStruct((PPD, LAGS), F32),...  51.6 us

profile of v7, /device:TPU:1, one launch (start us, length us, event | category | flops | bytes accessed | tf_op | source)
XLA Modules:
  0.0 52.3 jit_solution(8886396374831228502)
XLA Ops:
  0.0 51.6 %shard_map.64 = f32[48,2001]{1,0:T(8,128)S(1)} custom-call(bf16[16,2048]{1,0:T(8,128)(2,1)} %bitcast.7, s32[1,16]{1,0:T(1,128)} %bitcast.10, s32[1,16]{1,0:T(1,128)} %bitcast.11, s32[32,128]{1,0:T(8,128)} %bitcast.8, s32[64,384]{1,0:T(8,128)} %tiles_hbm.1, s32[2,48]{1,0:T(2,128)} %bitcast.9), custom_call_target="tpu_custom_call" | custom-call | tf_op jit(solution)/shard_map/pallas_call | solution.py:410
  51.6 0.7 %copy.8 = f32[1,1,48,2001]{3,2,1,0:T(8,128)} copy(f32[1,1,48,2001]{3,2,1,0:T(8,128)S(1)} %bitcast.6) | data formatting | bytes 768384
